TPU v7x, 128 devices: a whole 4x4x4 slice. The times are simulated.
128 devices in a mesh: group: 4 (over z_hi, core), dev: 32 (over y, z_lo, x).
Axes of the slice: x: 4, y: 4, z: 4 (z_hi: 2, z_lo: 2; z = z_hi * 2 + z_lo), core: 2. Of those that a mesh axis runs over, the one named last changes fastest.
Arguments:
- couplings: bfloat16 [128, 6, 4, 512, 512], P(('group', 'dev')), may hold values from -0.0625 to 0.0625
- history: bfloat16 [32, 65536, 256], P(None, ('group', 'dev')), may hold values from -6 to 6
- diag_inverse: bfloat16 [128, 512, 512], P(('group', 'dev')), may hold values from -0.25 to 0.25
- incident: bfloat16 [2, 65536, 256], P(None, ('group', 'dev')), may hold values from -6 to 6
- targets: int32 [128, 6], P(('group', 'dev')), may hold values from 0 to 10
- delays: int32 [128, 6], P(('group', 'dev')), may hold values from 1 to 29
- counts: int32 [128], P(('group', 'dev')), may hold values from 1 to 6, as said below
Outputs:
- currents: bfloat16 [2, 65536, 256], P(None, ('group', 'dev'))
Inputs may be any that keep to these rules, and one draw needn't show every extreme that they name: `counts`: slots beyond a block's count carry matrices that are not couplings. Some block uses all 6 slots.
All inputs are finite; a program needn't handle non-finite values.
Results may differ from a plain program's by a relative error of at most 0.0048.
Values sent between devices are 32-bit elements; how exact they have to be, the bound alone decides.
A program may use at most 128 MiB of HBM per device.

v0:
```python
import jax
import jax.numpy as jnp
from jax import lax
from jax.sharding import PartitionSpec as P

BAND = 4
STEPS = 2


target_codes = 11


def from_behind(value, axis, by):
    size = lax.axis_size(axis)
    pairs = [(i, i + by) for i in range(size) if 0 <= i + by < size]
    return lax.ppermute(value, axis, pairs)


def slot_terms(couplings, recent, targets, delays, counts):

    def take_band(lowest):
        return lax.dynamic_slice_in_dim(recent, lowest - 1, BAND, 0)

    slices = jax.vmap(take_band)(delays[0])
    product = jnp.einsum("cwij,cwjr->cir", couplings[0], slices, preferred_element_type=jnp.float32)
    live_slots = jnp.arange(couplings.shape[1]) < counts[0]
    onehot = (
        (targets[0][None, :] == jnp.arange(target_codes)[:, None]) & live_slots[None, :]
    ).astype(jnp.float32)
    return jnp.einsum("sc,cir->sir", onehot, product, precision=lax.Precision.HIGHEST)


def deliver(stencil):
    payloads = {}
    for grp_step in (1, -1):
        lowest = 5 if grp_step == 1 else 8
        payloads[grp_step] = stencil[lowest : lowest + 3]
    far_steps = (-2, -1, 1, 2)
    arrivals = []
    for grp_step in (1, -1):
        arrived = from_behind(payloads[grp_step], "group", grp_step)
        arrivals.append(arrived)
    near_terms = stencil[0:5]
    field_sum = stencil[2]
    for arrived in arrivals:
        field_sum = field_sum + arrived[1]
        for dev_step in (-1, 1):
            field_sum = field_sum + from_behind(arrived[dev_step + 1], "dev", dev_step)
    for dev_step in far_steps:
        field_sum = field_sum + from_behind(near_terms[dev_step + 2], "dev", dev_step)
    return field_sum


def shards(couplings, history, diag_inverse, incident, targets, delays, counts):
    recent = history
    outputs = []
    for moment in range(STEPS):
        stencil = slot_terms(couplings, recent, targets, delays, counts)
        field_sum = deliver(stencil)
        right_side = (incident[moment].astype(jnp.float32) - field_sum).astype(jnp.bfloat16)
        current = jnp.dot(diag_inverse[0], right_side, preferred_element_type=jnp.float32).astype(
            jnp.bfloat16
        )
        outputs.append(current)
        recent = jnp.concatenate([current[None], recent[:-1]], axis=0)
    return jnp.stack(outputs)


def solution(mesh):
    placed = (
        P(("group", "dev"), None, None, None, None),
        P(None, ("group", "dev"), None),
        P(("group", "dev"), None, None),
        P(None, ("group", "dev"), None),
        P(("group", "dev"), None),
        P(("group", "dev"), None),
        P(("group", "dev")),
    )
    return jax.shard_map(
        shards,
        mesh=mesh,
        in_specs=placed,
        out_specs=P(None, ("group", "dev"), None),
        check_vma=False,
    )
```

profile of v0, /device:TPU:25, one launch (start us, length us, event | category | flops | bytes accessed | tf_op | source)
XLA Modules:
  0.0 271.7 jit_solution(10458845409789233308)
XLA Ops:
  0.7 0.7 shift-left_bitcast_fusion
  1.4 12.0 %copy.8 = bf16[32,512,256]{1,2,0:T(8,128)(2,1)} copy(bf16[32,512,256]{2,1,0:T(8,128)(2,1)} %param.8) | data formatting | bytes 16777216 | tf_op args[1]
  13.4 7.6 %gather_fusion = bf16[6,4,512,256]{2,3,1,0:T(8,128)(2,1)} fusion(bf16[32,512,256]{1,2,0:T(8,128)(2,1)} %copy.8, s32[6]{0:T(128)S(1)} %shift-left_bitcast_fusion), kind=kCustom, calls=%fused_computation | custom fusion | bytes 12582984 | tf_op jit(solution)/shard_map/vmap()/gather | solution.py:22
  21.0 11.5 %fusion.2 = f32[6,256,512,1]{2,1,3,0:T(8,128)} fusion(bf16[6,4,512,256]{2,3,1,0:T(8,128)(2,1)} %gather_fusion, bf16[1,6,4,512,512]{4,3,2,1,0:T(8,128)(2,1)} %param.7), kind=kOutput, calls=%fused_computation.4 | convolution fusion | flops 3221225472 | bytes 22020096 | tf_op jit(solution)/shard_map/cwij,cwjr->cir/dot_general | solution.py:25
  32.4 5.2 %copy.23 = f32[6,256,512,1]{1,0,2,3:T(8,128)} copy(f32[6,256,512,1]{2,1,3,0:T(8,128)} %fusion.2) | data formatting | bytes 6291456 | tf_op jit(solution)/shard_map/cwij,cwjr->cir/dot_general | solution.py:25
  37.6 5.8 %fusion.6 = f32[11,512,256]{2,0,1:T(8,128)S(1)} fusion(f32[6,256,512,1]{1,0,2,3:T(8,128)} %copy.23, s32[6]{0:T(128)S(1)} %bitcast.167, pred[6]{0:T(512)(128)(4,1)S(1)} %iota_compare_fusion.1), kind=kOutput, calls=%fused_computation.9 | convolution fusion | flops 103809152 | bytes 8912926 | tf_op jit(solution)/shard_map/sc,cir->sir/dot_general | solution.py:30
  43.4 0.7 fusion.54
  44.1 0.3 copy.29
  44.4 2.6 collective-permute-start.3
  47.0 0.3 copy.28
  47.3 5.4 %collective-permute-start = (f32[3,512,256]{2,1,0:T(8,128)S(1)}, f32[3,512,256]{2,1,0:T(8,128)S(1)}, u32[]{:S(2)}, u32[]{:S(2)}) collective-permute-start(f32[3,512,256]{2,1,0:T(8,128)S(1)} %copy.28), channel_id=1, source_target_pairs={{0,32},{32,64},{64,96},{1,33},{33,65},{65,97},{2,34},{34,66},{66,9... | collective-permute-start | bytes 4718600 | tf_op jit(solution)/shard_map/ppermute | solution.py:16
  52.7 1.9 fusion.53
  54.6 3.1 %collective-permute-start.8 = (f32[512,256]{1,0:T(8,128)S(1)}, f32[512,256]{1,0:T(8,128)S(1)}, u32[]{:S(2)}, u32[]{:S(2)}) collective-permute-start(f32[512,256]{1,0:T(8,128)S(1)} %bitcast.165), channel_id=1, source_target_pairs={{0,1},{1,2},{2,3},{3,4},{4,5},{5,6},{6,7},{7,8},{8,9},{9,10},{10,1... | collective-permute-start | bytes 1572872 | tf_op jit(solution)/shard_map/ppermute | solution.py:16
  57.8 4.4 %collective-permute-start.9 = (f32[512,256]{1,0:T(8,128)S(1)}, f32[512,256]{1,0:T(8,128)S(1)}, u32[]{:S(2)}, u32[]{:S(2)}) collective-permute-start(f32[512,256]{1,0:T(8,128)S(1)} %bitcast.164), channel_id=1, source_target_pairs={{0,2},{1,3},{2,4},{3,5},{4,6},{5,7},{6,8},{7,9},{8,10},{9,11},{10,... | collective-permute-start | bytes 1572872 | tf_op jit(solution)/shard_map/ppermute | solution.py:16
  62.2 4.2 %collective-permute-start.6 = (f32[512,256]{1,0:T(8,128)S(1)}, f32[512,256]{1,0:T(8,128)S(1)}, u32[]{:S(2)}, u32[]{:S(2)}) collective-permute-start(f32[512,256]{1,0:T(8,128)S(1)} %bitcast.162), channel_id=1, source_target_pairs={{2,0},{3,1},{4,2},{5,3},{6,4},{7,5},{8,6},{9,7},{10,8},{11,9},{12,... | collective-permute-start | bytes 1572872 | tf_op jit(solution)/shard_map/ppermute | solution.py:16
  66.5 25.0 %collective-permute-done.3 = f32[3,512,256]{2,1,0:T(8,128)S(1)} collective-permute-done((f32[3,512,256]{2,1,0:T(8,128)S(1)}, f32[3,512,256]{2,1,0:T(8,128)S(1)}, u32[]{:S(2)}, u32[]{:S(2)}) %collective-permute-start.3) | collective-permute-done | bytes 1572896 | tf_op jit(solution)/shard_map/ppermute | solution.py:16
  91.5 1.9 collective-permute-start.7
  93.4 0.1 slice_bitcast_fusion.6
  93.5 21.5 %collective-permute-done = f32[3,512,256]{2,1,0:T(8,128)S(1)} collective-permute-done((f32[3,512,256]{2,1,0:T(8,128)S(1)}, f32[3,512,256]{2,1,0:T(8,128)S(1)}, u32[]{:S(2)}, u32[]{:S(2)}) %collective-permute-start) | collective-permute-done | bytes 1572896 | tf_op jit(solution)/shard_map/ppermute | solution.py:16
  115.0 1.9 collective-permute-start.4
  116.9 0.1 slice_bitcast_fusion.9
  117.0 0.0 collective-permute-done.8
  117.0 3.4 %collective-permute-start.5 = (f32[512,256]{1,0:T(8,128)S(1)}, f32[512,256]{1,0:T(8,128)}, u32[]{:S(2)}, u32[]{:S(2)}) collective-permute-start(f32[512,256]{1,0:T(8,128)S(1)} %get-tuple-element.26), channel_id=1, source_target_pairs={{0,1},{1,2},{2,3},{3,4},{4,5},{5,6},{6,7},{7,8},{8,9},{9,10},{10,1... | collective-permute-start | bytes 1572872 | tf_op jit(solution)/shard_map/ppermute | solution.py:16
  120.4 0.0 collective-permute-done.9
  120.4 4.9 %collective-permute-start.1 = (f32[512,256]{1,0:T(8,128)S(1)}, f32[512,256]{1,0:T(8,128)}, u32[]{:S(2)}, u32[]{:S(2)}) collective-permute-start(f32[512,256]{1,0:T(8,128)S(1)} %get-tuple-element.23), channel_id=1, source_target_pairs={{1,0},{2,1},{3,2},{4,3},{5,4},{6,5},{7,6},{8,7},{9,8},{10,9},{11,1... | collective-permute-start | bytes 1572872 | tf_op jit(solution)/shard_map/ppermute | solution.py:16
  125.3 0.0 collective-permute-done.6
  125.4 0.0 copy-start.1
  125.4 0.8 copy-done.1
  126.2 2.1 collective-permute-start.2
  128.3 7.3 %slice.145 = bf16[31,512,256]{1,2,0:T(8,128)(2,1)} slice(bf16[32,512,256]{1,2,0:T(8,128)(2,1)} %copy.8), slice={[0:31], [0:512], [0:256]} | slice | bytes 16252928 | tf_op jit(solution)/shard_map/slice | solution.py:65
  135.6 0.0 collective-permute-done.7
  135.6 0.0 collective-permute-done.4
  135.6 3.6 %collective-permute-done.2 = f32[512,256]{1,0:T(8,128)} collective-permute-done((f32[512,256]{1,0:T(8,128)S(1)}, f32[512,256]{1,0:T(8,128)}, u32[]{:S(2)}, u32[]{:S(2)}) %collective-permute-start.2) | collective-permute-done | bytes 524320 | tf_op jit(solution)/shard_map/ppermute | solution.py:16
  139.2 2.7 fusion.8
  141.9 7.3 %pad_maximum_fusion = bf16[32,512,256]{1,2,0:T(8,128)(2,1)} fusion(bf16[31,512,256]{1,2,0:T(8,128)(2,1)} %slice.145, bf16[1,512,256]{1,2,0:T(8,128)(2,1)S(1)} %fusion.8), kind=kLoop, calls=%fused_computation.6 | loop fusion | flops 4194304 | bytes 16777216 | tf_op jit(solution)/shard_map/concatenate | solution.py:65
  149.2 7.6 %gather_fusion.1 = bf16[6,4,512,256]{2,3,1,0:T(8,128)(2,1)} fusion(bf16[32,512,256]{1,2,0:T(8,128)(2,1)} %pad_maximum_fusion, s32[6]{0:T(128)S(1)} %shift-left_bitcast_fusion), kind=kCustom, calls=%fused_computation.1 | custom fusion | bytes 12582984 | tf_op jit(solution)/shard_map/vmap()/gather | solution.py:22
  156.7 11.5 %fusion = f32[6,256,512,1]{2,1,3,0:T(8,128)} fusion(bf16[6,4,512,256]{2,3,1,0:T(8,128)(2,1)} %gather_fusion.1, bf16[1,6,4,512,512]{4,3,2,1,0:T(8,128)(2,1)} %param.7), kind=kOutput, calls=%fused_computation.2 | convolution fusion | flops 3221225472 | bytes 22020096 | tf_op jit(solution)/shard_map/cwij,cwjr->cir/dot_general | solution.py:25
  168.2 5.1 %copy.24 = f32[6,256,512,1]{1,0,2,3:T(8,128)} copy(f32[6,256,512,1]{2,1,3,0:T(8,128)} %fusion) | data formatting | bytes 6291456 | tf_op jit(solution)/shard_map/cwij,cwjr->cir/dot_general | solution.py:25
  173.3 5.8 %fusion.4 = f32[11,512,256]{2,0,1:T(8,128)S(1)} fusion(f32[6,256,512,1]{1,0,2,3:T(8,128)} %copy.24, s32[6]{0:T(128)S(1)} %bitcast.168, pred[6]{0:T(512)(128)(4,1)S(1)} %iota_compare_fusion.1), kind=kOutput, calls=%fused_computation.7 | convolution fusion | flops 103809152 | bytes 8912926 | tf_op jit(solution)/shard_map/sc,cir->sir/dot_general | solution.py:30
  179.1 0.7 fusion.52
  179.8 0.3 copy.35
  180.1 1.9 collective-permute-start.13
  182.0 0.3 copy.34
  182.4 7.6 %collective-permute-start.10 = (f32[3,512,256]{2,1,0:T(8,128)S(1)}, f32[3,512,256]{2,1,0:T(8,128)S(1)}, u32[]{:S(2)}, u32[]{:S(2)}) collective-permute-start(f32[3,512,256]{2,1,0:T(8,128)S(1)} %copy.34), channel_id=1, source_target_pairs={{0,32},{32,64},{64,96},{1,33},{33,65},{65,97},{2,34},{34,66},{66,9... | collective-permute-start | bytes 4718600 | tf_op jit(solution)/shard_map/ppermute | solution.py:16
  190.0 1.9 fusion.51
  191.8 0.0 copy-start.2
  192.0 1.9 collective-permute-start.18
  194.0 1.9 collective-permute-start.19
  195.9 6.7 %collective-permute-start.16 = (f32[512,256]{1,0:T(8,128)S(1)}, f32[512,256]{1,0:T(8,128)S(1)}, u32[]{:S(2)}, u32[]{:S(2)}) collective-permute-start(f32[512,256]{1,0:T(8,128)S(1)} %bitcast.160), channel_id=1, source_target_pairs={{2,0},{3,1},{4,2},{5,3},{6,4},{7,5},{8,6},{9,7},{10,8},{11,9},{12,... | collective-permute-start | bytes 1572872 | tf_op jit(solution)/shard_map/ppermute | solution.py:16
  202.6 42.1 %collective-permute-done.13 = f32[3,512,256]{2,1,0:T(8,128)S(1)} collective-permute-done((f32[3,512,256]{2,1,0:T(8,128)S(1)}, f32[3,512,256]{2,1,0:T(8,128)S(1)}, u32[]{:S(2)}, u32[]{:S(2)}) %collective-permute-start.13) | collective-permute-done | bytes 1572896 | tf_op jit(solution)/shard_map/ppermute | solution.py:16
  244.7 1.9 collective-permute-start.17
  246.6 0.1 slice_bitcast_fusion.1
  246.7 1.9 collective-permute-start.14
  248.6 0.1 slice_bitcast_fusion.4
  248.7 3.4 %collective-permute-start.15 = (f32[512,256]{1,0:T(8,128)S(1)}, f32[512,256]{1,0:T(8,128)S(1)}, u32[]{:S(2)}, u32[]{:S(2)}) collective-permute-start(f32[512,256]{1,0:T(8,128)S(1)} %get-tuple-element.22), channel_id=1, source_target_pairs={{0,1},{1,2},{2,3},{3,4},{4,5},{5,6},{6,7},{7,8},{8,9},{9,10},{10,1... | collective-permute-start | bytes 1572872 | tf_op jit(solution)/shard_map/ppermute | solution.py:16
  252.1 4.9 %collective-permute-start.11 = (f32[512,256]{1,0:T(8,128)S(1)}, f32[512,256]{1,0:T(8,128)S(1)}, u32[]{:S(2)}, u32[]{:S(2)}) collective-permute-start(f32[512,256]{1,0:T(8,128)S(1)} %get-tuple-element.19), channel_id=1, source_target_pairs={{1,0},{2,1},{3,2},{4,3},{5,4},{6,5},{7,6},{8,7},{9,8},{10,9},{11,1... | collective-permute-start | bytes 1572872 | tf_op jit(solution)/shard_map/ppermute | solution.py:16
  257.0 1.9 collective-permute-start.12
  259.0 1.2 collective-permute-done.14
  260.2 1.4 collective-permute-done.15
  261.6 4.2 %collective-permute-done.11 = f32[512,256]{1,0:T(8,128)S(1)} collective-permute-done((f32[512,256]{1,0:T(8,128)S(1)}, f32[512,256]{1,0:T(8,128)S(1)}, u32[]{:S(2)}, u32[]{:S(2)}) %collective-permute-start.11) | collective-permute-done | bytes 524320 | tf_op jit(solution)/shard_map/ppermute | solution.py:16
  265.8 4.1 %collective-permute-done.12 = f32[512,256]{1,0:T(8,128)S(1)} collective-permute-done((f32[512,256]{1,0:T(8,128)S(1)}, f32[512,256]{1,0:T(8,128)S(1)}, u32[]{:S(2)}, u32[]{:S(2)}) %collective-permute-start.12) | collective-permute-done | bytes 524320 | tf_op jit(solution)/shard_map/ppermute | solution.py:16
  270.0 0.6 fusion.9
  270.6 0.1 pad_maximum_fusion.1
  270.7 1.0 copy.22
  (21 shorter events, 0.3 us)
Async XLA Ops:
  0.0 139.2 %copy-start = (bf16[1,512,512]{2,1,0:T(8,128)(2,1)S(1)}, bf16[1,512,512]{2,1,0:T(8,128)(2,1)}, u32[]{:S(2)}) copy-start(bf16[1,512,512]{2,1,0:T(8,128)(2,1)} %param.9) | copy-start | bytes 1572868
  32.4 5.2 %copy-start.3 = (s32[1,6]{1,0:T(1,128)S(1)}, s32[1,6]{1,0:T(1,128)}, u32[]{:S(2)}) copy-start(s32[1,6]{1,0:T(1,128)} %param.11) | copy-start | bytes 76
  44.4 47.1 %collective-permute-start.3 = (f32[3,512,256]{2,1,0:T(8,128)S(1)}, f32[3,512,256]{2,1,0:T(8,128)S(1)}, u32[]{:S(2)}, u32[]{:S(2)}) collective-permute-start(f32[3,512,256]{2,1,0:T(8,128)S(1)} %copy.29), channel_id=1, source_target_pairs={{32,0},{64,32},{96,64},{33,1},{65,33},{97,65},{34,2},{66,34},{98,6... | collective-permute-start | bytes 4718600 | tf_op jit(solution)/shard_map/ppermute | solution.py:16
  47.3 67.7 %collective-permute-start = (f32[3,512,256]{2,1,0:T(8,128)S(1)}, f32[3,512,256]{2,1,0:T(8,128)S(1)}, u32[]{:S(2)}, u32[]{:S(2)}) collective-permute-start(f32[3,512,256]{2,1,0:T(8,128)S(1)} %copy.28), channel_id=1, source_target_pairs={{0,32},{32,64},{64,96},{1,33},{33,65},{65,97},{2,34},{34,66},{66,9... | collective-permute-start | bytes 4718600 | tf_op jit(solution)/shard_map/ppermute | solution.py:16
  54.6 62.4 %collective-permute-start.8 = (f32[512,256]{1,0:T(8,128)S(1)}, f32[512,256]{1,0:T(8,128)S(1)}, u32[]{:S(2)}, u32[]{:S(2)}) collective-permute-start(f32[512,256]{1,0:T(8,128)S(1)} %bitcast.165), channel_id=1, source_target_pairs={{0,1},{1,2},{2,3},{3,4},{4,5},{5,6},{6,7},{7,8},{8,9},{9,10},{10,1... | collective-permute-start | bytes 1572872 | tf_op jit(solution)/shard_map/ppermute | solution.py:16
  57.8 62.6 %collective-permute-start.9 = (f32[512,256]{1,0:T(8,128)S(1)}, f32[512,256]{1,0:T(8,128)S(1)}, u32[]{:S(2)}, u32[]{:S(2)}) collective-permute-start(f32[512,256]{1,0:T(8,128)S(1)} %bitcast.164), channel_id=1, source_target_pairs={{0,2},{1,3},{2,4},{3,5},{4,6},{5,7},{6,8},{7,9},{8,10},{9,11},{10,... | collective-permute-start | bytes 1572872 | tf_op jit(solution)/shard_map/ppermute | solution.py:16
  62.2 63.1 %collective-permute-start.6 = (f32[512,256]{1,0:T(8,128)S(1)}, f32[512,256]{1,0:T(8,128)S(1)}, u32[]{:S(2)}, u32[]{:S(2)}) collective-permute-start(f32[512,256]{1,0:T(8,128)S(1)} %bitcast.162), channel_id=1, source_target_pairs={{2,0},{3,1},{4,2},{5,3},{6,4},{7,5},{8,6},{9,7},{10,8},{11,9},{12,... | collective-permute-start | bytes 1572872 | tf_op jit(solution)/shard_map/ppermute | solution.py:16
  91.5 44.1 %collective-permute-start.7 = (f32[512,256]{1,0:T(8,128)S(1)}, f32[512,256]{1,0:T(8,128)}, u32[]{:S(2)}, u32[]{:S(2)}) collective-permute-start(f32[512,256]{1,0:T(8,128)S(1)} %bitcast.161), channel_id=1, source_target_pairs={{1,0},{2,1},{3,2},{4,3},{5,4},{6,5},{7,6},{8,7},{9,8},{10,9},{11,1... | collective-permute-start | bytes 1572872 | tf_op jit(solution)/shard_map/ppermute | solution.py:16
  115.0 20.5 %collective-permute-start.4 = (f32[512,256]{1,0:T(8,128)S(1)}, f32[512,256]{1,0:T(8,128)}, u32[]{:S(2)}, u32[]{:S(2)}) collective-permute-start(f32[512,256]{1,0:T(8,128)S(1)} %get-tuple-element.25), channel_id=1, source_target_pairs={{1,0},{2,1},{3,2},{4,3},{5,4},{6,5},{7,6},{8,7},{9,8},{10,9},{11,1... | collective-permute-start | bytes 1572872 | tf_op jit(solution)/shard_map/ppermute | solution.py:16
  117.0 18.5 %collective-permute-start.5 = (f32[512,256]{1,0:T(8,128)S(1)}, f32[512,256]{1,0:T(8,128)}, u32[]{:S(2)}, u32[]{:S(2)}) collective-permute-start(f32[512,256]{1,0:T(8,128)S(1)} %get-tuple-element.26), channel_id=1, source_target_pairs={{0,1},{1,2},{2,3},{3,4},{4,5},{5,6},{6,7},{7,8},{8,9},{9,10},{10,1... | collective-permute-start | bytes 1572872 | tf_op jit(solution)/shard_map/ppermute | solution.py:16
  120.4 15.2 %collective-permute-start.1 = (f32[512,256]{1,0:T(8,128)S(1)}, f32[512,256]{1,0:T(8,128)}, u32[]{:S(2)}, u32[]{:S(2)}) collective-permute-start(f32[512,256]{1,0:T(8,128)S(1)} %get-tuple-element.23), channel_id=1, source_target_pairs={{1,0},{2,1},{3,2},{4,3},{5,4},{6,5},{7,6},{8,7},{9,8},{10,9},{11,1... | collective-permute-start | bytes 1572872 | tf_op jit(solution)/shard_map/ppermute | solution.py:16
  125.4 0.8 copy-start.1
  126.2 13.0 %collective-permute-start.2 = (f32[512,256]{1,0:T(8,128)S(1)}, f32[512,256]{1,0:T(8,128)}, u32[]{:S(2)}, u32[]{:S(2)}) collective-permute-start(f32[512,256]{1,0:T(8,128)S(1)} %get-tuple-element.24), channel_id=1, source_target_pairs={{0,1},{1,2},{2,3},{3,4},{4,5},{5,6},{6,7},{7,8},{8,9},{9,10},{10,1... | collective-permute-start | bytes 1572872 | tf_op jit(solution)/shard_map/ppermute | solution.py:16
  180.1 64.6 %collective-permute-start.13 = (f32[3,512,256]{2,1,0:T(8,128)S(1)}, f32[3,512,256]{2,1,0:T(8,128)S(1)}, u32[]{:S(2)}, u32[]{:S(2)}) collective-permute-start(f32[3,512,256]{2,1,0:T(8,128)S(1)} %copy.35), channel_id=1, source_target_pairs={{32,0},{64,32},{96,64},{33,1},{65,33},{97,65},{34,2},{66,34},{98,6... | collective-permute-start | bytes 4718600 | tf_op jit(solution)/shard_map/ppermute | solution.py:16
  182.4 64.3 %collective-permute-start.10 = (f32[3,512,256]{2,1,0:T(8,128)S(1)}, f32[3,512,256]{2,1,0:T(8,128)S(1)}, u32[]{:S(2)}, u32[]{:S(2)}) collective-permute-start(f32[3,512,256]{2,1,0:T(8,128)S(1)} %copy.34), channel_id=1, source_target_pairs={{0,32},{32,64},{64,96},{1,33},{33,65},{65,97},{2,34},{34,66},{66,9... | collective-permute-start | bytes 4718600 | tf_op jit(solution)/shard_map/ppermute | solution.py:16
  191.8 78.1 %copy-start.2 = (bf16[2,512,256]{2,1,0:T(8,128)(2,1)S(1)}, bf16[2,512,256]{2,1,0:T(8,128)(2,1)}, u32[]{:S(2)}) copy-start(bf16[2,512,256]{2,1,0:T(8,128)(2,1)} %param.10) | copy-start | bytes 1572868
  192.0 56.7 %collective-permute-start.18 = (f32[512,256]{1,0:T(8,128)S(1)}, f32[512,256]{1,0:T(8,128)S(1)}, u32[]{:S(2)}, u32[]{:S(2)}) collective-permute-start(f32[512,256]{1,0:T(8,128)S(1)} %bitcast.166), channel_id=1, source_target_pairs={{0,1},{1,2},{2,3},{3,4},{4,5},{5,6},{6,7},{7,8},{8,9},{9,10},{10,1... | collective-permute-start | bytes 1572872 | tf_op jit(solution)/shard_map/ppermute | solution.py:16
  194.0 58.1 %collective-permute-start.19 = (f32[512,256]{1,0:T(8,128)S(1)}, f32[512,256]{1,0:T(8,128)S(1)}, u32[]{:S(2)}, u32[]{:S(2)}) collective-permute-start(f32[512,256]{1,0:T(8,128)S(1)} %bitcast.163), channel_id=1, source_target_pairs={{0,2},{1,3},{2,4},{3,5},{4,6},{5,7},{6,8},{7,9},{8,10},{9,11},{10,... | collective-permute-start | bytes 1572872 | tf_op jit(solution)/shard_map/ppermute | solution.py:16
  195.9 61.1 %collective-permute-start.16 = (f32[512,256]{1,0:T(8,128)S(1)}, f32[512,256]{1,0:T(8,128)S(1)}, u32[]{:S(2)}, u32[]{:S(2)}) collective-permute-start(f32[512,256]{1,0:T(8,128)S(1)} %bitcast.160), channel_id=1, source_target_pairs={{2,0},{3,1},{4,2},{5,3},{6,4},{7,5},{8,6},{9,7},{10,8},{11,9},{12,... | collective-permute-start | bytes 1572872 | tf_op jit(solution)/shard_map/ppermute | solution.py:16
  244.7 14.3 %collective-permute-start.17 = (f32[512,256]{1,0:T(8,128)S(1)}, f32[512,256]{1,0:T(8,128)S(1)}, u32[]{:S(2)}, u32[]{:S(2)}) collective-permute-start(f32[512,256]{1,0:T(8,128)S(1)} %bitcast.159), channel_id=1, source_target_pairs={{1,0},{2,1},{3,2},{4,3},{5,4},{6,5},{7,6},{8,7},{9,8},{10,9},{11,1... | collective-permute-start | bytes 1572872 | tf_op jit(solution)/shard_map/ppermute | solution.py:16
  246.7 13.5 %collective-permute-start.14 = (f32[512,256]{1,0:T(8,128)S(1)}, f32[512,256]{1,0:T(8,128)S(1)}, u32[]{:S(2)}, u32[]{:S(2)}) collective-permute-start(f32[512,256]{1,0:T(8,128)S(1)} %get-tuple-element.21), channel_id=1, source_target_pairs={{1,0},{2,1},{3,2},{4,3},{5,4},{6,5},{7,6},{8,7},{9,8},{10,9},{11,1... | collective-permute-start | bytes 1572872 | tf_op jit(solution)/shard_map/ppermute | solution.py:16
  248.7 12.9 %collective-permute-start.15 = (f32[512,256]{1,0:T(8,128)S(1)}, f32[512,256]{1,0:T(8,128)S(1)}, u32[]{:S(2)}, u32[]{:S(2)}) collective-permute-start(f32[512,256]{1,0:T(8,128)S(1)} %get-tuple-element.22), channel_id=1, source_target_pairs={{0,1},{1,2},{2,3},{3,4},{4,5},{5,6},{6,7},{7,8},{8,9},{9,10},{10,1... | collective-permute-start | bytes 1572872 | tf_op jit(solution)/shard_map/ppermute | solution.py:16
  252.1 13.7 %collective-permute-start.11 = (f32[512,256]{1,0:T(8,128)S(1)}, f32[512,256]{1,0:T(8,128)S(1)}, u32[]{:S(2)}, u32[]{:S(2)}) collective-permute-start(f32[512,256]{1,0:T(8,128)S(1)} %get-tuple-element.19), channel_id=1, source_target_pairs={{1,0},{2,1},{3,2},{4,3},{5,4},{6,5},{7,6},{8,7},{9,8},{10,9},{11,1... | collective-permute-start | bytes 1572872 | tf_op jit(solution)/shard_map/ppermute | solution.py:16
  257.0 12.9 %collective-permute-start.12 = (f32[512,256]{1,0:T(8,128)S(1)}, f32[512,256]{1,0:T(8,128)S(1)}, u32[]{:S(2)}, u32[]{:S(2)}) collective-permute-start(f32[512,256]{1,0:T(8,128)S(1)} %get-tuple-element.20), channel_id=1, source_target_pairs={{0,1},{1,2},{2,3},{3,4},{4,5},{5,6},{6,7},{7,8},{8,9},{9,10},{10,1... | collective-permute-start | bytes 1572872 | tf_op jit(solution)/shard_map/ppermute | solution.py:16
where the time goes:
time: 273 us; the launch traced here: 272 us
  waiting for transfers between devices  103 us (38%)
  starting transfers between devices  68 us (25%)
  local copies, waits for them, and re-layouts  53.4 us (20%)
  matrix products  37.8 us (14%)
  other arithmetic  8.02 us (3%)
    ppermute x20, waiting for transfers between devices, from_behind(): return lax.ppermute(value, axis, pairs)  103 us
    ppermute x20, starting transfers between devices, from_behind(): return lax.ppermute(value, axis, pairs)  68 us
    dot_general x2, matrix products, slot_terms(): jnp.einsum('cwij,cwjr->cir', couplings[0], slices, preferred_element_type...  23 us
    gather x2, local copies, waits for them, and re-layouts, take_band(): return lax.dynamic_slice_in_dim(recent, lowest - 1, BAND, 0)  15.1 us
    unnamed x21, local copies, waits for them, and re-layouts  14.3 us
    dot_general x2, matrix products, slot_terms(): jnp.einsum('sc,cir->sir', onehot, product, precision=lax.Precision.HIGHEST)  11.5 us
    dot_general x2, local copies, waits for them, and re-layouts, slot_terms(): jnp.einsum('cwij,cwjr->cir', couplings[0], slices, preferred_element_type...  10.2 us
    slice x1, local copies, waits for them, and re-layouts, shards(): recent = jnp.concatenate([current[None], recent[:-1]], axis=0)  7.31 us
  transfers between devices with their start and end apart: 20, of which 8 were waited for; matrix products, arithmetic and copies ran while one was open for 4% of the time, Pallas kernels for 0%

commit v1 on v0

v1 whole, which is shorter than its diff:
```python
import functools

import jax
import jax.numpy as jnp
from jax import lax
from jax.experimental import pallas as pl
from jax.experimental.pallas import tpu as pltpu
from jax.sharding import PartitionSpec as P

BAND = 4
STEPS = 2
LANES = 128
MESH = pl.DeviceIdType.MESH

FAR_R, FAR_L, UP, DOWN, SUM_R, SUM_L = 0, 1, 2, 5, 8, 9
KINDS = 10


def march_kernel(
    n_group,
    n_dev,
    targets,
    delays,
    counts,
    couplings,
    history,
    diag,
    incident,
    out,
    past,
    mats,
    solve,
    shine,
    product,
    terms,
    gated,
    far,
    near,
    cross,
    load_sem,
    mat_sem,
    send_sem,
    recv_sem,
):
    g = lax.axis_index("group")
    d = lax.axis_index("dev")
    slots = mats.shape[0]
    unk = mats.shape[2]
    halves = terms.shape[1]
    tile = min(unk, 128)
    has_up, has_down = g < n_group - 1, g > 0
    has_right, has_left = d < n_dev - 1, d > 0

    loads = [
        pltpu.make_async_copy(history.at[pl.ds(0, past.shape[0] - 1)], past.at[pl.ds(1, past.shape[0] - 1)], load_sem.at[0]),
        pltpu.make_async_copy(diag.at[0], solve, load_sem.at[1]),
        pltpu.make_async_copy(incident, shine, load_sem.at[2]),
    ]
    loads[0].start()

    def mat_load(c):
        return pltpu.make_async_copy(couplings.at[0, c], mats.at[c], mat_sem.at[c])

    @pl.loop(0, slots)
    def _(c):
        mat_load(c).start()

    loads[1].start()
    loads[2].start()

    barrier = pltpu.get_barrier_semaphore()
    partners = (
        (has_up, (g + 1, d)),
        (has_down, (g - 1, d)),
        (has_right, (g, d + 1)),
        (has_left, (g, d - 1)),
    )
    greeted = jnp.int32(0)
    for there, where in partners:

        @pl.when(there)
        def _():
            pl.semaphore_signal(barrier, inc=1, device_id=where, device_id_type=MESH)

        greeted = greeted + there.astype(jnp.int32)

    past[0] = jnp.zeros_like(past[0])
    gated[0] = jnp.zeros_like(gated[0])
    for side, absent in ((0, jnp.logical_not(has_down)), (1, jnp.logical_not(has_up))):

        @pl.when(absent)
        def _():
            for t in range(STEPS):
                for h in range(halves):
                    cross[t, h, side] = jnp.zeros_like(cross[t, h, side])

    for side, absent in ((0, jnp.logical_not(has_left)), (1, jnp.logical_not(has_right))):

        @pl.when(absent)
        def _():
            for t in range(STEPS):
                for h in range(halves):
                    far[t, h, side] = jnp.zeros_like(far[t, h, side])
                    near[t, h, side] = jnp.zeros_like(near[t, h, side])

    def remote(src, dst, t, h, kind, where):
        return pltpu.make_async_remote_copy(
            src_ref=src,
            dst_ref=dst,
            send_sem=send_sem.at[t, h, kind],
            recv_sem=recv_sem.at[t, h, kind],
            device_id=where,
            device_id_type=MESH,
        )

    def copies(t, h):
        st = terms.at[t, h]
        plan = {
            FAR_R: (remote(st.at[4], far.at[t, h, 0], t, h, FAR_R, (g, d + 1)), d < n_dev - 2, (d >= 1) & (d < n_dev - 1)),
            FAR_L: (remote(st.at[0], far.at[t, h, 1], t, h, FAR_L, (g, d - 1)), d >= 2, (d >= 1) & (d < n_dev - 1)),
            SUM_R: (remote(st.at[3], near.at[t, h, 0], t, h, SUM_R, (g, d + 1)), has_right, has_left),
            SUM_L: (remote(st.at[1], near.at[t, h, 1], t, h, SUM_L, (g, d - 1)), has_left, has_right),
        }
        for k in range(3):
            plan[UP + k] = (remote(st.at[5 + k], cross.at[t, h, 0, k], t, h, UP + k, (g + 1, d)), has_up, has_down)
            plan[DOWN + k] = (remote(st.at[8 + k], cross.at[t, h, 1, k], t, h, DOWN + k, (g - 1, d)), has_down, has_up)
        return plan

    plans = {(t, h): copies(t, h) for t in range(STEPS) for h in range(halves)}

    def send(t, h, kind):
        copy, sends, _ = plans[t, h][kind]

        @pl.when(sends)
        def _():
            copy.start()

    def arrive(t, h, kind):
        copy, _, hears = plans[t, h][kind]

        @pl.when(hears)
        def _():
            copy.wait_recv()

    live = [(jnp.int32(c) < counts[0]) for c in range(slots)]

    def weight(s, c):
        return jnp.where(live[c] & (targets[0, c] == s), 1.0, 0.0).astype(jnp.float32)

    def gather_terms(t, h, codes):
        weights = {s: [weight(s, c) for c in range(slots)] for s in codes}

        @pl.loop(0, unk // tile)
        def _(r):
            rows = pl.ds(pl.multiple_of(r * tile, tile), tile)
            parts = [product[c, h, rows, :] for c in range(slots)]
            for s in codes:
                total = parts[0] * weights[s][0]
                for c in range(1, slots):
                    total = total + parts[c] * weights[s][c]
                terms[t, h, s, rows, :] = total

    def launch(t, h):
        for codes, kinds in (
            ((4, 0), (FAR_R, FAR_L)),
            ((5, 7), (UP, UP + 2)),
            ((8, 10), (DOWN, DOWN + 2)),
            ((6, 9), (UP + 1, DOWN + 1)),
        ):
            gather_terms(t, h, codes)
            for kind in kinds:
                send(t, h, kind)
        gather_terms(t, h, (3, 1, 2))

    def products(shift):
        @pl.loop(0, slots)
        def _(c):
            if shift:
                mat_load(c).wait()
            first = jnp.maximum(delays[0, c], 1) - 1 + shift
            total = jnp.dot(mats[c, 0], past[first], preferred_element_type=jnp.float32)
            for w in range(1, BAND):
                total = total + jnp.dot(mats[c, w], past[first + w], preferred_element_type=jnp.float32)
            for h in range(halves):
                product[c, h] = total[:, h * LANES : (h + 1) * LANES]

    def pass_on(t, h):
        arrive(t, h, FAR_R)
        arrive(t, h, UP + 2)
        arrive(t, h, DOWN + 2)

        @pl.when(has_right)
        def _():
            terms[t, h, 3] = terms[t, h, 3] + cross[t, h, 0, 2] + cross[t, h, 1, 2] + far[t, h, 0]

        send(t, h, SUM_R)
        arrive(t, h, FAR_L)
        arrive(t, h, UP)
        arrive(t, h, DOWN)

        @pl.when(has_left)
        def _():
            terms[t, h, 1] = terms[t, h, 1] + cross[t, h, 0, 0] + cross[t, h, 1, 0] + far[t, h, 1]

        send(t, h, SUM_L)

    def finish(t, h):
        cols = pl.ds(h * LANES, LANES)
        for kind in (UP + 1, DOWN + 1, SUM_R, SUM_L):
            arrive(t, h, kind)
        field = terms[t, h, 2] + cross[t, h, 0, 1] + cross[t, h, 1, 1] + near[t, h, 0] + near[t, h, 1]
        right_side = (shine[t, :, cols].astype(jnp.float32) - field).astype(jnp.bfloat16)
        current = jnp.dot(solve[...], right_side, preferred_element_type=jnp.float32).astype(jnp.bfloat16)
        out[t, :, cols] = current
        if t == 0:
            gated[1] = current

            @pl.loop(0, slots)
            def _(c):
                fresh = jnp.where(delays[0, c] == 1, 1, 0)
                product[c, h] = product[c, h] + jnp.dot(mats[c, 0], gated[fresh], preferred_element_type=jnp.float32)

    loads[0].wait()
    pl.semaphore_wait(barrier, greeted)
    products(1)
    for h in range(halves):
        launch(0, h)
    products(0)
    for h in range(halves):
        pass_on(0, h)
    loads[1].wait()
    loads[2].wait()
    for h in range(halves):
        finish(0, h)
        launch(1, h)
    for h in range(halves):
        pass_on(1, h)
    for h in range(halves):
        finish(1, h)
    for plan in plans.values():
        for copy, sends, _ in plan.values():

            @pl.when(sends)
            def _():
                copy.wait_send()


def march(n_group, n_dev, couplings, history, diag_inverse, incident, targets, delays, counts):
    _, slots, band, unk, _ = couplings.shape
    hist, _, exc = history.shape
    halves = exc // LANES
    smem = pl.BlockSpec(memory_space=pltpu.SMEM)
    hbm = pl.BlockSpec(memory_space=pl.ANY)
    block = (unk, LANES)
    return pl.pallas_call(
        functools.partial(march_kernel, n_group, n_dev),
        out_shape=jax.ShapeDtypeStruct((STEPS, unk, exc), jnp.bfloat16),
        in_specs=[smem, smem, smem, hbm, hbm, hbm, hbm],
        out_specs=pl.BlockSpec(memory_space=pltpu.VMEM),
        scratch_shapes=[
            pltpu.VMEM((hist + 1, unk, exc), jnp.bfloat16),
            pltpu.VMEM((slots, band, unk, unk), jnp.bfloat16),
            pltpu.VMEM((unk, unk), jnp.bfloat16),
            pltpu.VMEM((STEPS, unk, exc), jnp.bfloat16),
            pltpu.VMEM((slots, halves) + block, jnp.float32),
            pltpu.VMEM((STEPS, halves, 11) + block, jnp.float32),
            pltpu.VMEM((2,) + block, jnp.bfloat16),
            pltpu.VMEM((STEPS, halves, 2) + block, jnp.float32),
            pltpu.VMEM((STEPS, halves, 2) + block, jnp.float32),
            pltpu.VMEM((STEPS, halves, 2, 3) + block, jnp.float32),
            pltpu.SemaphoreType.DMA((3,)),
            pltpu.SemaphoreType.DMA((slots,)),
            pltpu.SemaphoreType.DMA((STEPS, halves, KINDS)),
            pltpu.SemaphoreType.DMA((STEPS, halves, KINDS)),
        ],
        compiler_params=pltpu.CompilerParams(
            collective_id=0, has_side_effects=True, vmem_limit_bytes=62 * 2**20
        ),
        name="march",
    )(targets, delays, counts, couplings, history, diag_inverse, incident)


def solution(mesh):
    placed = (
        P(("group", "dev"), None, None, None, None),
        P(None, ("group", "dev"), None),
        P(("group", "dev"), None, None),
        P(None, ("group", "dev"), None),
        P(("group", "dev"), None),
        P(("group", "dev"), None),
        P(("group", "dev")),
    )
    return jax.shard_map(
        functools.partial(march, mesh.shape["group"], mesh.shape["dev"]),
        mesh=mesh,
        in_specs=placed,
        out_specs=P(None, ("group", "dev"), None),
        check_vma=False,
    )
```

time: 273 us -> 105 us (0.38)
  the two profiles are of different devices: /device:TPU:25 before, /device:TPU:80 now
where the time goes in v1:
time: 105 us
  Pallas kernels  103 us (98%)
  local copies, waits for them, and re-layouts  1.87 us (2%)
    pallas_call x1, Pallas kernels, march(): pl.pallas_call(functools.partial(march_kernel, n_group, n_dev), out_shape...  103 us

profile of v1, /device:TPU:80, one launch (start us, length us, event | category | flops | bytes accessed | tf_op | source)
XLA Modules:
  0.0 105.3 jit_solution(15839808191980597606)
XLA Ops:
  0.7 102.8 %march.1 = bf16[2,512,256]{2,1,0:T(8,128)(2,1)} custom-call(s32[1,6]{1,0:T(1,128)} %targets.1, s32[1,6]{1,0:T(1,128)} %delays.1, s32[1]{0:T(128)S(6)} %copy.9.counts, bf16[1,6,4,512,512]{4,3,2,1,0:T(8,128)(2,1)} %couplings.1, bf16[32,512,256]{2,1,0:T(8,128)(2,1)} %history.1, bf16[1,512,512]{2,1,0:T(8,128)(2,1)} %diag.1, bf16[2,512,256]{2,1,0:T(8,128)(2,1)} %incident.1), custom_call_target="tpu_custom_call" | custom-call | tf_op jit(solution)/shard_map/march/pallas_call | solution.py:255
  103.5 1.9 %copy.10 = bf16[2,512,256]{2,1,0:T(8,128)(2,1)} copy(bf16[2,512,256]{2,1,0:T(8,128)(2,1)} %march.1) | data formatting | bytes 1048576

commit v2 on v1

v2 whole, which is shorter than its diff:
```python
import functools

import jax
import jax.numpy as jnp
from jax import lax
from jax.experimental import pallas as pl
from jax.experimental.pallas import tpu as pltpu
from jax.sharding import PartitionSpec as P

BAND = 4
STEPS = 2
LANES = 128
RUN = 4
MESH = pl.DeviceIdType.MESH

FAR_R, FAR_L, SUM_R, SUM_L, CHIP, JOIN, SKIP, MIDDLE = range(8)
KINDS = 8


def march_kernel(
    n_dev,
    run,
    targets,
    delays,
    counts,
    couplings,
    history,
    diag,
    incident,
    out,
    past,
    mats,
    solve,
    shine,
    product,
    terms,
    gated,
    box,
    chip_box,
    load_sem,
    mat_sem,
    send_sem,
    recv_sem,
):
    g = lax.axis_index("group")
    d = lax.axis_index("dev")
    slots = mats.shape[0]
    unk = mats.shape[2]
    halves = terms.shape[1]
    tile = min(unk, 128)
    has_right, has_left = d < n_dev - 1, d > 0
    mate = g + 1 - 2 * (g % 2)
    crosses = (g == 1) | (g == 2)
    over = 3 - g
    x = d % run
    chip_code = 5 + 3 * (g % 2)
    over_code = 5 + 3 * (g // 2)
    even = x % 2 == 0
    join_code = over_code + jnp.where(even, 2, 0)
    skip_code = over_code + jnp.where(even, 0, 2)
    join_dev = d + jnp.where(even, 1, -1)
    at_start, at_end = x == 0, x == run - 1
    skip_dev = d + jnp.where(at_start, -1, 0) + jnp.where(at_end, 1, 0)
    skips = crosses & (skip_dev >= 0) & (skip_dev < n_dev)
    at_rim = at_start | at_end
    skip_into = jnp.where(at_rim, 2, jnp.where(even, 1, 3))

    depth = past.shape[0] - 1
    loads = [
        pltpu.make_async_copy(history, past.at[pl.ds(1, depth)], load_sem.at[0]),
        pltpu.make_async_copy(diag.at[0], solve, load_sem.at[1]),
        pltpu.make_async_copy(incident, shine, load_sem.at[2]),
    ]
    loads[0].start()

    def mat_load(c):
        return pltpu.make_async_copy(couplings.at[0, c], mats.at[c], mat_sem.at[c])

    @pl.loop(0, slots)
    def _(c):
        mat_load(c).start()

    loads[1].start()
    loads[2].start()

    barrier = pltpu.get_barrier_semaphore()
    greeted = jnp.int32(1)
    pl.semaphore_signal(barrier, inc=1, device_id=(mate, d), device_id_type=MESH)
    for there, where in (
        (has_right, (g, d + 1)),
        (has_left, (g, d - 1)),
        (crosses, (over, d)),
        (skips & at_rim, (over, skip_dev)),
    ):

        @pl.when(there)
        def _():
            pl.semaphore_signal(barrier, inc=1, device_id=where, device_id_type=MESH)

        greeted = greeted + there.astype(jnp.int32)

    past[0] = jnp.zeros_like(past[0])
    gated[0] = jnp.zeros_like(gated[0])

    def remote(src, dst, t, h, kind, where):
        return pltpu.make_async_remote_copy(
            src_ref=src,
            dst_ref=dst,
            send_sem=send_sem.at[t, h, kind],
            recv_sem=recv_sem.at[t, h, kind],
            device_id=where,
            device_id_type=MESH,
        )

    def copies(t, h):
        def one(code, kind, where, sends, hears):
            return remote(terms.at[t, h, code], box.at[t, h, kind], t, h, kind, where), sends, hears

        inner = has_right & has_left
        chip = remote(terms.at[t, h, pl.ds(chip_code, 3)], chip_box.at[t, h], t, h, CHIP, (mate, d))
        return {
            FAR_R: one(4, FAR_R, (g, d + 1), d < n_dev - 2, inner),
            FAR_L: one(0, FAR_L, (g, d - 1), d >= 2, inner),
            SUM_R: one(3, SUM_R, (g, d + 1), has_right, has_left),
            SUM_L: one(1, SUM_L, (g, d - 1), has_left, has_right),
            CHIP: (chip, None, None),
            JOIN: one(join_code, JOIN, (g, join_dev), crosses, crosses),
            SKIP: one(skip_code, SKIP, (over, skip_dev), skips, skips),
            MIDDLE: one(over_code + 1, MIDDLE, (over, d), crosses, crosses),
        }

    plans = {(t, h): copies(t, h) for t in range(STEPS) for h in range(halves)}

    def when(there, do):
        if there is None:
            do()
        else:
            pl.when(there)(do)

    def send(t, h, kind):
        copy, sends, _ = plans[t, h][kind]
        when(sends, copy.start)

    def arrive(t, h, kind):
        copy, _, hears = plans[t, h][kind]
        when(hears, copy.wait_recv)

    live = [(jnp.int32(c) < counts[0]) for c in range(slots)]

    def weight(s, c):
        return jnp.where(live[c] & (targets[0, c] == s), 1.0, 0.0).astype(jnp.float32)

    def gather_terms(t, h, codes):
        weights = {s: [weight(s, c) for c in range(slots)] for s in codes}

        @pl.loop(0, unk // tile)
        def _(r):
            rows = pl.ds(pl.multiple_of(r * tile, tile), tile)
            parts = [product[c, h, rows, :] for c in range(slots)]
            for s in codes:
                total = parts[0] * weights[s][0]
                for c in range(1, slots):
                    total = total + parts[c] * weights[s][c]
                terms[t, h, s, rows, :] = total

    def launch(t, h):
        gather_terms(t, h, (4, 0))
        send(t, h, FAR_R)
        send(t, h, FAR_L)
        gather_terms(t, h, (5, 6, 7))
        gather_terms(t, h, (8, 9, 10))
        for kind in (JOIN, SKIP, CHIP):
            send(t, h, kind)
        gather_terms(t, h, (3, 1, 2))

    def products(shift):
        @pl.loop(0, slots)
        def _(c):
            if shift:
                mat_load(c).wait()
            first = jnp.maximum(delays[0, c], 1) - 1 + shift
            total = jnp.dot(mats[c, 0], past[first], preferred_element_type=jnp.float32)
            for w in range(1, BAND):
                total = total + jnp.dot(mats[c, w], past[first + w], preferred_element_type=jnp.float32)
            for h in range(halves):
                product[c, h] = total[:, h * LANES : (h + 1) * LANES]

    def add(t, h, code, kind, there):
        def do():
            terms[t, h, code] = terms[t, h, code] + box[t, h, kind]

        when(there, do)

    def pass_on(t, h):
        arrive(t, h, JOIN)
        add(t, h, over_code + 1, JOIN, crosses)
        send(t, h, MIDDLE)
        arrive(t, h, CHIP)
        arrive(t, h, SKIP)
        add(t, h, skip_into, SKIP, skips)
        for code, far_kind, sum_kind, sends in ((3, FAR_R, SUM_R, has_right), (1, FAR_L, SUM_L, has_left)):
            arrive(t, h, far_kind)
            terms[t, h, code] = terms[t, h, code] + chip_box[t, h, code - 1]
            add(t, h, code, far_kind, has_right & has_left)
            send(t, h, sum_kind)

    def finish(t, h):
        cols = pl.ds(h * LANES, LANES)
        terms[t, h, 2] = terms[t, h, 2] + chip_box[t, h, 1]
        for kind, there in ((MIDDLE, crosses), (SUM_R, has_left), (SUM_L, has_right)):
            arrive(t, h, kind)
            add(t, h, 2, kind, there)
        right_side = (shine[t, :, cols].astype(jnp.float32) - terms[t, h, 2]).astype(jnp.bfloat16)
        current = jnp.dot(solve[...], right_side, preferred_element_type=jnp.float32).astype(jnp.bfloat16)
        out[t, :, cols] = current
        if t == 0:
            gated[1] = current

            @pl.loop(0, slots)
            def _(c):
                fresh = jnp.where(delays[0, c] == 1, 1, 0)
                product[c, h] = product[c, h] + jnp.dot(mats[c, 0], gated[fresh], preferred_element_type=jnp.float32)

    loads[0].wait()
    pl.semaphore_wait(barrier, greeted)
    products(1)
    for h in range(halves):
        launch(0, h)
    products(0)
    for h in range(halves):
        pass_on(0, h)
    loads[1].wait()
    loads[2].wait()
    for h in range(halves):
        finish(0, h)
        launch(1, h)
    for h in range(halves):
        pass_on(1, h)
    for h in range(halves):
        finish(1, h)
    for plan in plans.values():
        for copy, sends, _ in plan.values():
            when(sends, copy.wait_send)


def march(n_dev, couplings, history, diag_inverse, incident, targets, delays, counts):
    _, slots, band, unk, _ = couplings.shape
    hist, _, exc = history.shape
    halves = exc // LANES
    smem = pl.BlockSpec(memory_space=pltpu.SMEM)
    hbm = pl.BlockSpec(memory_space=pl.ANY)
    block = (unk, LANES)
    return pl.pallas_call(
        functools.partial(march_kernel, n_dev, RUN),
        out_shape=jax.ShapeDtypeStruct((STEPS, unk, exc), jnp.bfloat16),
        in_specs=[smem, smem, smem, hbm, hbm, hbm, hbm],
        out_specs=pl.BlockSpec(memory_space=pltpu.VMEM),
        scratch_shapes=[
            pltpu.VMEM((hist + 1, unk, exc), jnp.bfloat16),
            pltpu.VMEM((slots, band, unk, unk), jnp.bfloat16),
            pltpu.VMEM((unk, unk), jnp.bfloat16),
            pltpu.VMEM((STEPS, unk, exc), jnp.bfloat16),
            pltpu.VMEM((slots, halves) + block, jnp.float32),
            pltpu.VMEM((STEPS, halves, 11) + block, jnp.float32),
            pltpu.VMEM((2,) + block, jnp.bfloat16),
            pltpu.VMEM((STEPS, halves, KINDS) + block, jnp.float32),
            pltpu.VMEM((STEPS, halves, 3) + block, jnp.float32),
            pltpu.SemaphoreType.DMA((3,)),
            pltpu.SemaphoreType.DMA((slots,)),
            pltpu.SemaphoreType.DMA((STEPS, halves, KINDS)),
            pltpu.SemaphoreType.DMA((STEPS, halves, KINDS)),
        ],
        compiler_params=pltpu.CompilerParams(
            collective_id=0, has_side_effects=True, vmem_limit_bytes=62 * 2**20
        ),
        name="march",
    )(targets, delays, counts, couplings, history, diag_inverse, incident)


def solution(mesh):
    placed = (
        P(("group", "dev"), None, None, None, None),
        P(None, ("group", "dev"), None),
        P(("group", "dev"), None, None),
        P(None, ("group", "dev"), None),
        P(("group", "dev"), None),
        P(("group", "dev"), None),
        P(("group", "dev")),
    )
    return jax.shard_map(
        functools.partial(march, mesh.shape["dev"]),
        mesh=mesh,
        in_specs=placed,
        out_specs=P(None, ("group", "dev"), None),
        check_vma=False,
    )
```

time: 105 us -> 84.4 us (0.80)
  the two profiles are of different devices: /device:TPU:80 before, /device:TPU:25 now
where the time goes in v2:
time: 84.4 us; the launch traced here: 83.3 us
  Pallas kernels  80.8 us (96%)
  local copies, waits for them, and re-layouts  1.87 us (2%)
    pallas_call x1, Pallas kernels, march(): pl.pallas_call(functools.partial(march_kernel, n_dev, RUN), out_shape=jax...  80.8 us
    unnamed x1, local copies, waits for them, and re-layouts  1.87 us

profile of v2, /device:TPU:25, one launch (start us, length us, event | category | flops | bytes accessed | tf_op | source)
XLA Modules:
  0.0 83.3 jit_solution(15295119426113290854)
XLA Ops:
  0.7 80.8 %march.1 = bf16[2,512,256]{2,1,0:T(8,128)(2,1)} custom-call(s32[1,6]{1,0:T(1,128)} %targets.1, s32[1,6]{1,0:T(1,128)} %delays.1, s32[1]{0:T(128)S(6)} %copy.9.counts, bf16[1,6,4,512,512]{4,3,2,1,0:T(8,128)(2,1)} %couplings.1, bf16[32,512,256]{2,1,0:T(8,128)(2,1)} %history.1, bf16[1,512,512]{2,1,0:T(8,128)(2,1)} %diag.1, bf16[2,512,256]{2,1,0:T(8,128)(2,1)} %incident.1), custom_call_target="tpu_custom_call" | custom-call | tf_op jit(solution)/shard_map/march/pallas_call | solution.py:253
  81.4 1.9 %copy.10 = bf16[2,512,256]{2,1,0:T(8,128)(2,1)} copy(bf16[2,512,256]{2,1,0:T(8,128)(2,1)} %march.1) | data formatting | bytes 1048576

commit v3 on v2

v3 whole, which is shorter than its diff:
```python
import functools

import jax
import jax.numpy as jnp
from jax import lax
from jax.experimental import pallas as pl
from jax.experimental.pallas import tpu as pltpu
from jax.sharding import PartitionSpec as P

BAND = 4
STEPS = 2
LANES = 128
TILE = 128
RUN = 4
MESH = pl.DeviceIdType.MESH

FAR, SUM, CHIP, JOIN, SKIP, MIDDLE = 0, 2, 4, 5, 6, 7
KINDS = 8


def march_kernel(
    n_dev,
    run,
    targets,
    delays,
    counts,
    couplings,
    history,
    diag,
    incident,
    out,
    past_0,
    past_1,
    mats,
    solve,
    shine,
    product,
    terms,
    gated,
    box,
    chip_box,
    load_sem,
    mat_sem,
    send_sem,
    recv_sem,
):
    g = lax.axis_index("group")
    d = lax.axis_index("dev")
    slots = mats.shape[0]
    unk = mats.shape[2]
    halves = terms.shape[1]
    tiles = unk // TILE
    has_right, has_left = d < n_dev - 1, d > 0
    mate = g + 1 - 2 * (g % 2)
    crosses = (g == 1) | (g == 2)
    over = 3 - g
    x = d % run
    chip_code = 5 + 3 * (g % 2)
    over_code = 5 + 3 * (g // 2)
    even = x % 2 == 0
    join_code = over_code + jnp.where(even, 2, 0)
    skip_code = over_code + jnp.where(even, 0, 2)
    join_dev = d + jnp.where(even, 1, -1)
    at_start, at_end = x == 0, x == run - 1
    skip_dev = d + jnp.where(at_start, -1, 0) + jnp.where(at_end, 1, 0)
    skips = crosses & (skip_dev >= 0) & (skip_dev < n_dev)
    at_rim = at_start | at_end
    near_side = jnp.where(at_start, 1, 0)
    skip_into = jnp.where(at_rim, 2, jnp.where(even, 1, 3))

    def tile_rows(r):
        return pl.ds(pl.multiple_of(r * TILE, TILE), TILE)

    past = (past_0, past_1)
    depth = past_0.shape[0] - 1

    def history_load(h):
        cols = pl.ds(h * LANES, LANES)
        return pltpu.make_async_copy(history.at[:, :, cols], past[h].at[pl.ds(1, depth)], load_sem.at[h])

    solve_load = pltpu.make_async_copy(diag.at[0], solve, load_sem.at[halves])
    shine_load = pltpu.make_async_copy(incident, shine, load_sem.at[halves + 1])

    def mat_load(r):
        rows = tile_rows(r)
        return pltpu.make_async_copy(couplings.at[0, :, :, rows, :], mats.at[:, :, rows, :], mat_sem.at[r])

    history_load(0).start()
    mat_load(0).start()
    for h in range(1, halves):
        history_load(h).start()

    @pl.loop(1, tiles)
    def _(r):
        mat_load(r).start()

    solve_load.start()
    shine_load.start()

    barrier = pltpu.get_barrier_semaphore()
    greeted = jnp.int32(1)
    pl.semaphore_signal(barrier, inc=1, device_id=(mate, d), device_id_type=MESH)
    for there, where in (
        (has_right, (g, d + 1)),
        (has_left, (g, d - 1)),
        (crosses, (over, d)),
        (skips & at_rim, (over, skip_dev)),
    ):

        @pl.when(there)
        def _():
            pl.semaphore_signal(barrier, inc=1, device_id=where, device_id_type=MESH)

        greeted = greeted + there.astype(jnp.int32)

    for held in past:
        held[0] = jnp.zeros_like(held[0])
    gated[0] = jnp.zeros_like(gated[0])

    def copy_of(t, h, r, kind, side=0):
        code_is_chip = kind == CHIP
        inner = has_right & has_left
        aside = d + 1 - 2 * side
        beyond = aside + 1 - 2 * side
        inside = (aside >= 0) & (aside < n_dev)
        behind = d - 1 + 2 * side
        code, where, sends, hears = {
            FAR: (4 - 4 * side, (g, aside), (beyond >= 0) & (beyond < n_dev), inner),
            SUM: (3 - 2 * side, (g, aside), inside, (behind >= 0) & (behind < n_dev)),
            CHIP: (pl.ds(chip_code, 3), (mate, d), None, None),
            JOIN: (join_code, (g, join_dev), crosses, crosses),
            SKIP: (skip_code, (over, skip_dev), skips, skips),
            MIDDLE: (over_code + 1, (over, d), crosses, crosses),
        }[kind]
        rows = tile_rows(r)
        kind = kind + side
        target = chip_box.at[t, h, :, rows] if code_is_chip else box.at[t, h, kind, rows]
        copy = pltpu.make_async_remote_copy(
            src_ref=terms.at[t, h, code, rows],
            dst_ref=target,
            send_sem=send_sem.at[t, h, kind, r],
            recv_sem=recv_sem.at[t, h, kind, r],
            device_id=where,
            device_id_type=MESH,
        )
        return copy, sends, hears

    def when(there, do):
        if there is None:
            do()
        else:
            pl.when(there)(do)

    def send(t, h, r, kind, side=0):
        copy, sends, _ = copy_of(t, h, r, kind, side)
        when(sends, copy.start)

    def arrive(t, h, r, kind, side=0):
        copy, _, hears = copy_of(t, h, r, kind, side)
        when(hears, copy.wait_recv)

    live = [(jnp.int32(c) < counts[0]) for c in range(slots)]

    def weight(s, c):
        return jnp.where(live[c] & (targets[0, c] == s), 1.0, 0.0).astype(jnp.float32)

    weights = [[weight(s, c) for c in range(slots)] for s in range(11)]

    def gather_terms(t, h, r, codes):
        rows = tile_rows(r)
        parts = [product[c, h, rows, :] for c in range(slots)]
        for s in codes:
            total = parts[0] * weights[s][0]
            for c in range(1, slots):
                total = total + parts[c] * weights[s][c]
            terms[t, h, s, rows, :] = total

    def launch(t, h, r):
        gather_terms(t, h, r, (5, 6, 7))
        gather_terms(t, h, r, (8, 9, 10))
        for kind in (JOIN, SKIP, CHIP):
            send(t, h, r, kind)
        gather_terms(t, h, r, (4, 0))
        for side in (0, 1):
            send(t, h, r, FAR, side)
        gather_terms(t, h, r, (3, 1, 2))

    def first_of(c):
        return jnp.maximum(delays[0, c], 1) - 1

    def products(shift, rows, over_halves):
        def taken(at):
            return jnp.concatenate([past[h][at] for h in over_halves], axis=1)

        @pl.loop(0, slots)
        def _(c):
            first = first_of(c) + shift
            total = jnp.dot(mats[c, 0, rows], taken(first), preferred_element_type=jnp.float32)
            for w in range(1, BAND):
                total = total + jnp.dot(mats[c, w, rows], taken(first + w), preferred_element_type=jnp.float32)
            for i, h in enumerate(over_halves):
                product[c, h, rows, :] = total[:, i * LANES : (i + 1) * LANES]

    def add(t, h, r, code, kind, there):
        rows = tile_rows(r)

        def do():
            terms[t, h, code, rows] = terms[t, h, code, rows] + box[t, h, kind, rows]

        when(there, do)

    def join(t, h, r):
        arrive(t, h, r, JOIN)
        add(t, h, r, over_code + 1, JOIN, crosses)
        send(t, h, r, MIDDLE)

    def pass_on(t, h, r):
        rows = tile_rows(r)
        arrive(t, h, r, CHIP)
        arrive(t, h, r, SKIP)
        add(t, h, r, skip_into, SKIP, skips)
        for side in (near_side, 1 - near_side):
            code = 3 - 2 * side
            arrive(t, h, r, FAR, side)
            terms[t, h, code, rows] = terms[t, h, code, rows] + chip_box[t, h, code - 1, rows]
            add(t, h, r, code, FAR + side, has_right & has_left)
            send(t, h, r, SUM, side)

    def solve_step(t, h):
        cols = pl.ds(h * LANES, LANES)

        @pl.loop(0, tiles)
        def _(r):
            rows = tile_rows(r)
            terms[t, h, 2, rows] = terms[t, h, 2, rows] + chip_box[t, h, 1, rows]
            for kind, side, there in ((MIDDLE, 0, crosses), (SUM, 0, has_left), (SUM, 1, has_right)):
                arrive(t, h, r, kind, side)
                add(t, h, r, 2, kind + side, there)

        right_side = (shine[t, :, cols].astype(jnp.float32) - terms[t, h, 2]).astype(jnp.bfloat16)
        current = jnp.dot(solve[...], right_side, preferred_element_type=jnp.float32).astype(jnp.bfloat16)
        out[t, :, cols] = current
        if t == 0:
            gated[1] = current

    def refresh(h, rows):
        @pl.loop(0, slots)
        def _(c):
            fresh = jnp.where(delays[0, c] == 1, 1, 0)
            product[c, h, rows] = product[c, h, rows] + jnp.dot(mats[c, 0, rows], gated[fresh], preferred_element_type=jnp.float32)

    every = list(range(halves))
    history_load(0).wait()
    mat_load(0).wait()
    products(1, tile_rows(0), every[:1])
    pl.semaphore_wait(barrier, greeted)
    launch(0, 0, 0)
    for h in every[1:]:
        history_load(h).wait()
        products(1, tile_rows(0), [h])
        launch(0, h, 0)

    @pl.loop(1, tiles)
    def _(r):
        mat_load(r).wait()
        products(1, tile_rows(r), every)
        for h in every:
            launch(0, h, r)
            join(0, h, r - 1)

    for h in every:
        join(0, h, tiles - 1)

    @pl.loop(0, tiles)
    def _(r):
        pass_on(0, 0, r)
        products(0, tile_rows(r), every)

    for h in every[1:]:

        @pl.loop(0, tiles)
        def _(r):
            pass_on(0, h, r)

    solve_load.wait()
    shine_load.wait()
    for h in every:
        solve_step(0, h)

        @pl.loop(0, tiles)
        def _(r):
            refresh(h, tile_rows(r))
            launch(1, h, r)

            @pl.when(r > 0)
            def _():
                join(1, h, r - 1)

            if h:
                pass_on(1, h - 1, r)

        join(1, h, tiles - 1)

    @pl.loop(0, tiles)
    def _(r):
        pass_on(1, halves - 1, r)

    for h in every:
        solve_step(1, h)
    for t in range(STEPS):
        for h in range(halves):

            @pl.loop(0, tiles)
            def _(r):
                for kind, side in ((FAR, 0), (FAR, 1), (SUM, 0), (SUM, 1), (CHIP, 0), (JOIN, 0), (SKIP, 0), (MIDDLE, 0)):
                    copy, sends, _ = copy_of(t, h, r, kind, side)
                    when(sends, copy.wait_send)


def march(n_dev, couplings, history, diag_inverse, incident, targets, delays, counts):
    _, slots, band, unk, _ = couplings.shape
    hist, _, exc = history.shape
    halves = exc // LANES
    smem = pl.BlockSpec(memory_space=pltpu.SMEM)
    hbm = pl.BlockSpec(memory_space=pl.ANY)
    block = (unk, LANES)
    return pl.pallas_call(
        functools.partial(march_kernel, n_dev, RUN),
        out_shape=jax.ShapeDtypeStruct((STEPS, unk, exc), jnp.bfloat16),
        in_specs=[smem, smem, smem, hbm, hbm, hbm, hbm],
        out_specs=pl.BlockSpec(memory_space=pltpu.VMEM),
        scratch_shapes=[
            pltpu.VMEM((hist + 1,) + block, jnp.bfloat16),
            pltpu.VMEM((hist + 1,) + block, jnp.bfloat16),
            pltpu.VMEM((slots, band, unk, unk), jnp.bfloat16),
            pltpu.VMEM((unk, unk), jnp.bfloat16),
            pltpu.VMEM((STEPS, unk, exc), jnp.bfloat16),
            pltpu.VMEM((slots, halves) + block, jnp.float32),
            pltpu.VMEM((STEPS, halves, 11) + block, jnp.float32),
            pltpu.VMEM((2,) + block, jnp.bfloat16),
            pltpu.VMEM((STEPS, halves, KINDS) + block, jnp.float32),
            pltpu.VMEM((STEPS, halves, 3) + block, jnp.float32),
            pltpu.SemaphoreType.DMA((halves + 2,)),
            pltpu.SemaphoreType.DMA((unk // TILE,)),
            pltpu.SemaphoreType.DMA((STEPS, halves, KINDS, unk // TILE)),
            pltpu.SemaphoreType.DMA((STEPS, halves, KINDS, unk // TILE)),
        ],
        compiler_params=pltpu.CompilerParams(
            collective_id=0, has_side_effects=True, vmem_limit_bytes=62 * 2**20
        ),
        name="march",
    )(targets, delays, counts, couplings, history, diag_inverse, incident)


def solution(mesh):
    placed = (
        P(("group", "dev"), None, None, None, None),
        P(None, ("group", "dev"), None),
        P(("group", "dev"), None, None),
        P(None, ("group", "dev"), None),
        P(("group", "dev"), None),
        P(("group", "dev"), None),
        P(("group", "dev")),
    )
    return jax.shard_map(
        functools.partial(march, mesh.shape["dev"]),
        mesh=mesh,
        in_specs=placed,
        out_specs=P(None, ("group", "dev"), None),
        check_vma=False,
    )
```

time: 84.4 us -> 80 us (0.948); the launches traced: 83.3 us -> 79.8 us
  Pallas kernels: 80.8 us -> 77.3 us
    pallas_call x1, Pallas kernels: 80.8 us -> 77.3 us  [march(): pl.pallas_call(functools.partial(march_kernel, n_dev, RUN), out_shape=jax...]
where the time goes in v3:
time: 80 us; the launch traced here: 79.8 us
  Pallas kernels  77.3 us (97%)
  local copies, waits for them, and re-layouts  1.87 us (2%)
    pallas_call x1, Pallas kernels, march(): pl.pallas_call(functools.partial(march_kernel, n_dev, RUN), out_shape=jax...  77.3 us
    unnamed x1, local copies, waits for them, and re-layouts  1.87 us

profile of v3, /device:TPU:25, one launch (start us, length us, event | category | flops | bytes accessed | tf_op | source)
XLA Modules:
  0.0 79.8 jit_solution(479014910581769690)
XLA Ops:
  0.7 77.3 %march.1 = bf16[2,512,256]{2,1,0:T(8,128)(2,1)} custom-call(s32[1,6]{1,0:T(1,128)} %targets.1, s32[1,6]{1,0:T(1,128)} %delays.1, s32[1]{0:T(128)S(6)} %copy.9.counts, bf16[1,6,4,512,512]{4,3,2,1,0:T(8,128)(2,1)} %couplings.1, bf16[32,512,256]{2,1,0:T(8,128)(2,1)} %history.1, bf16[1,512,512]{2,1,0:T(8,128)(2,1)} %diag.1, bf16[2,512,256]{2,1,0:T(8,128)(2,1)} %incident.1), custom_call_target="tpu_custom_call" | custom-call | tf_op jit(solution)/shard_map/march/pallas_call | solution.py:327
  78.0 1.9 %copy.10 = bf16[2,512,256]{2,1,0:T(8,128)(2,1)} copy(bf16[2,512,256]{2,1,0:T(8,128)(2,1)} %march.1) | data formatting | bytes 1048576

commit v4 on v3

--- a/solution.py
+++ b/solution.py
@@ -14,8 +14,8 @@
 RUN = 4
 MESH = pl.DeviceIdType.MESH
 
-FAR, SUM, CHIP, JOIN, SKIP, MIDDLE = 0, 2, 4, 5, 6, 7
-KINDS = 8
+FAR, SUM, CHIP, JOIN, SKIP, MIDDLE, SIDE = 0, 2, 4, 5, 6, 7, 8
+KINDS = 9
 
 
 def march_kernel(
@@ -58,13 +58,17 @@
     chip_code = 5 + 3 * (g % 2)
     over_code = 5 + 3 * (g // 2)
     even = x % 2 == 0
+    at_start, at_end = x == 0, x == run - 1
+    at_rim = at_start | at_end
     join_code = over_code + jnp.where(even, 2, 0)
     skip_code = over_code + jnp.where(even, 0, 2)
-    join_dev = d + jnp.where(even, 1, -1)
-    at_start, at_end = x == 0, x == run - 1
-    skip_dev = d + jnp.where(at_start, -1, 0) + jnp.where(at_end, 1, 0)
+    join_group = jnp.where(at_rim, g, over)
+    join_dev = d + jnp.where(at_start, 1, 0) - jnp.where(at_end, 1, 0)
+    skip_dev = d - jnp.where(at_start, 1, 0) + jnp.where(at_end, 1, 0)
     skips = crosses & (skip_dev >= 0) & (skip_dev < n_dev)
-    at_rim = at_start | at_end
+    gathers = crosses & jnp.logical_not(at_rim)
+    skip_into = jnp.where(at_rim, 2, jnp.where(even, 1, 3))
+    side_into = jnp.where(even, 3, 1)
     near_side = jnp.where(at_start, 1, 0)
     skip_into = jnp.where(at_rim, 2, jnp.where(even, 1, 3))
 
@@ -117,7 +121,7 @@
         held[0] = jnp.zeros_like(held[0])
     gated[0] = jnp.zeros_like(gated[0])
 
-    def copy_of(t, h, r, kind, side=0):
+    def copy_of(t, h, r, kind, side=0, leaving=False):
         code_is_chip = kind == CHIP
         inner = has_right & has_left
         aside = d + 1 - 2 * side
@@ -128,12 +132,13 @@
             FAR: (4 - 4 * side, (g, aside), (beyond >= 0) & (beyond < n_dev), inner),
             SUM: (3 - 2 * side, (g, aside), inside, (behind >= 0) & (behind < n_dev)),
             CHIP: (pl.ds(chip_code, 3), (mate, d), None, None),
-            JOIN: (join_code, (g, join_dev), crosses, crosses),
+            JOIN: (join_code, (join_group, join_dev), crosses, gathers),
+            SIDE: (join_code, (join_group, join_dev), crosses, gathers),
             SKIP: (skip_code, (over, skip_dev), skips, skips),
             MIDDLE: (over_code + 1, (over, d), crosses, crosses),
         }[kind]
         rows = tile_rows(r)
-        kind = kind + side
+        kind = jnp.where(at_rim, JOIN, SIDE) if leaving and kind == JOIN else kind + side
         target = chip_box.at[t, h, :, rows] if code_is_chip else box.at[t, h, kind, rows]
         copy = pltpu.make_async_remote_copy(
             src_ref=terms.at[t, h, code, rows],
@@ -152,7 +157,7 @@
             pl.when(there)(do)
 
     def send(t, h, r, kind, side=0):
-        copy, sends, _ = copy_of(t, h, r, kind, side)
+        copy, sends, _ = copy_of(t, h, r, kind, side, True)
         when(sends, copy.start)
 
     def arrive(t, h, r, kind, side=0):
@@ -180,6 +185,11 @@
         gather_terms(t, h, r, (8, 9, 10))
         for kind in (JOIN, SKIP, CHIP):
             send(t, h, r, kind)
+
+        @pl.when(at_rim)
+        def _():
+            send(t, h, r, MIDDLE)
+
         gather_terms(t, h, r, (4, 0))
         for side in (0, 1):
             send(t, h, r, FAR, side)
@@ -210,15 +220,19 @@
         when(there, do)
 
     def join(t, h, r):
-        arrive(t, h, r, JOIN)
-        add(t, h, r, over_code + 1, JOIN, crosses)
-        send(t, h, r, MIDDLE)
+        @pl.when(gathers)
+        def _():
+            arrive(t, h, r, JOIN)
+            add(t, h, r, over_code + 1, JOIN, None)
+            send(t, h, r, MIDDLE)
 
     def pass_on(t, h, r):
         rows = tile_rows(r)
         arrive(t, h, r, CHIP)
         arrive(t, h, r, SKIP)
         add(t, h, r, skip_into, SKIP, skips)
+        arrive(t, h, r, SIDE)
+        add(t, h, r, side_into, SIDE, gathers)
         for side in (near_side, 1 - near_side):
             code = 3 - 2 * side
             arrive(t, h, r, FAR, side)
@@ -313,7 +327,7 @@
             @pl.loop(0, tiles)
             def _(r):
                 for kind, side in ((FAR, 0), (FAR, 1), (SUM, 0), (SUM, 1), (CHIP, 0), (JOIN, 0), (SKIP, 0), (MIDDLE, 0)):
-                    copy, sends, _ = copy_of(t, h, r, kind, side)
+                    copy, sends, _ = copy_of(t, h, r, kind, side, True)
                     when(sends, copy.wait_send)
 
 

time: 80 us -> 76.7 us (0.959)
  Pallas kernels: 77.3 us -> 74 us
    pallas_call x1, Pallas kernels: 77.3 us -> 74 us  [march(): pl.pallas_call(functools.partial(march_kernel, n_dev, RUN), out_shape=jax...]
where the time goes in v4:
time: 76.7 us; the launch traced here: 76.5 us
  Pallas kernels  74 us (96%)
  local copies, waits for them, and re-layouts  1.87 us (2%)
    pallas_call x1, Pallas kernels, march(): pl.pallas_call(functools.partial(march_kernel, n_dev, RUN), out_shape=jax...  74 us
    unnamed x1, local copies, waits for them, and re-layouts  1.87 us

profile of v4, /device:TPU:25, one launch (start us, length us, event | category | flops | bytes accessed | tf_op | source)
XLA Modules:
  0.0 76.5 jit_solution(3340605899077290041)
XLA Ops:
  0.7 74.0 %march.1 = bf16[2,512,256]{2,1,0:T(8,128)(2,1)} custom-call(s32[1,6]{1,0:T(1,128)} %targets.1, s32[1,6]{1,0:T(1,128)} %delays.1, s32[1]{0:T(128)S(6)} %copy.9.counts, bf16[1,6,4,512,512]{4,3,2,1,0:T(8,128)(2,1)} %couplings.1, bf16[32,512,256]{2,1,0:T(8,128)(2,1)} %history.1, bf16[1,512,512]{2,1,0:T(8,128)(2,1)} %diag.1, bf16[2,512,256]{2,1,0:T(8,128)(2,1)} %incident.1), custom_call_target="tpu_custom_call" | custom-call | tf_op jit(solution)/shard_map/march/pallas_call | solution.py:341
  74.6 1.9 %copy.10 = bf16[2,512,256]{2,1,0:T(8,128)(2,1)} copy(bf16[2,512,256]{2,1,0:T(8,128)(2,1)} %march.1) | data formatting | bytes 1048576

commit v5 on v4

--- a/solution.py
+++ b/solution.py
@@ -36,13 +36,16 @@
     shine,
     product,
     terms,
-    gated,
+    current_box,
     box,
     chip_box,
+    solved,
+    result,
     load_sem,
     mat_sem,
     send_sem,
     recv_sem,
+    out_sem,
 ):
     g = lax.axis_index("group")
     d = lax.axis_index("dev")
@@ -119,7 +122,6 @@
 
     for held in past:
         held[0] = jnp.zeros_like(held[0])
-    gated[0] = jnp.zeros_like(gated[0])
 
     def copy_of(t, h, r, kind, side=0, leaving=False):
         code_is_chip = kind == CHIP
@@ -242,6 +244,7 @@
 
     def solve_step(t, h):
         cols = pl.ds(h * LANES, LANES)
+        solved[...] = jnp.zeros_like(solved)
 
         @pl.loop(0, tiles)
         def _(r):
@@ -250,18 +253,25 @@
             for kind, side, there in ((MIDDLE, 0, crosses), (SUM, 0, has_left), (SUM, 1, has_right)):
                 arrive(t, h, r, kind, side)
                 add(t, h, r, 2, kind + side, there)
-
-        right_side = (shine[t, :, cols].astype(jnp.float32) - terms[t, h, 2]).astype(jnp.bfloat16)
-        current = jnp.dot(solve[...], right_side, preferred_element_type=jnp.float32).astype(jnp.bfloat16)
-        out[t, :, cols] = current
+            right_side = (shine[t, rows, cols].astype(jnp.float32) - terms[t, h, 2, rows]).astype(jnp.bfloat16)
+            solved[...] += jnp.dot(solve[:, rows], right_side, preferred_element_type=jnp.float32)
+
+        current = solved[...].astype(jnp.bfloat16)
+        result[t, h] = current
+        out_copy(t, h).start()
         if t == 0:
-            gated[1] = current
+            current_box[...] = current
+
+    def out_copy(t, h):
+        return pltpu.make_async_copy(result.at[t, h], out.at[t, :, pl.ds(h * LANES, LANES)], out_sem.at[t, h])
+
+    fresh = [jnp.where(delays[0, c] == 1, 1.0, 0.0).astype(jnp.float32) for c in range(slots)]
 
     def refresh(h, rows):
-        @pl.loop(0, slots)
-        def _(c):
-            fresh = jnp.where(delays[0, c] == 1, 1, 0)
-            product[c, h, rows] = product[c, h, rows] + jnp.dot(mats[c, 0, rows], gated[fresh], preferred_element_type=jnp.float32)
+        lead = mats[:, 0, rows, :].reshape(slots * TILE, unk)
+        newest = jnp.dot(lead, current_box[...], preferred_element_type=jnp.float32)
+        for c in range(slots):
+            product[c, h, rows] = product[c, h, rows] + newest[c * TILE : (c + 1) * TILE] * fresh[c]
 
     every = list(range(halves))
     history_load(0).wait()
@@ -288,7 +298,7 @@
     @pl.loop(0, tiles)
     def _(r):
         pass_on(0, 0, r)
-        products(0, tile_rows(r), every)
+
 
     for h in every[1:]:
 
@@ -296,6 +306,7 @@
         def _(r):
             pass_on(0, h, r)
 
+    products(0, pl.ds(0, unk), every)
     solve_load.wait()
     shine_load.wait()
     for h in every:
@@ -329,6 +340,8 @@
                 for kind, side in ((FAR, 0), (FAR, 1), (SUM, 0), (SUM, 1), (CHIP, 0), (JOIN, 0), (SKIP, 0), (MIDDLE, 0)):
                     copy, sends, _ = copy_of(t, h, r, kind, side, True)
                     when(sends, copy.wait_send)
+
+            out_copy(t, h).wait()
 
 
 def march(n_dev, couplings, history, diag_inverse, incident, targets, delays, counts):
@@ -342,7 +355,7 @@
         functools.partial(march_kernel, n_dev, RUN),
         out_shape=jax.ShapeDtypeStruct((STEPS, unk, exc), jnp.bfloat16),
         in_specs=[smem, smem, smem, hbm, hbm, hbm, hbm],
-        out_specs=pl.BlockSpec(memory_space=pltpu.VMEM),
+        out_specs=hbm,
         scratch_shapes=[
             pltpu.VMEM((hist + 1,) + block, jnp.bfloat16),
             pltpu.VMEM((hist + 1,) + block, jnp.bfloat16),
@@ -351,13 +364,16 @@
             pltpu.VMEM((STEPS, unk, exc), jnp.bfloat16),
             pltpu.VMEM((slots, halves) + block, jnp.float32),
             pltpu.VMEM((STEPS, halves, 11) + block, jnp.float32),
-            pltpu.VMEM((2,) + block, jnp.bfloat16),
+            pltpu.VMEM(block, jnp.bfloat16),
             pltpu.VMEM((STEPS, halves, KINDS) + block, jnp.float32),
             pltpu.VMEM((STEPS, halves, 3) + block, jnp.float32),
+            pltpu.VMEM(block, jnp.float32),
+            pltpu.VMEM((STEPS, halves) + block, jnp.bfloat16),
             pltpu.SemaphoreType.DMA((halves + 2,)),
             pltpu.SemaphoreType.DMA((unk // TILE,)),
             pltpu.SemaphoreType.DMA((STEPS, halves, KINDS, unk // TILE)),
             pltpu.SemaphoreType.DMA((STEPS, halves, KINDS, unk // TILE)),
+            pltpu.SemaphoreType.DMA((STEPS, halves)),
         ],
         compiler_params=pltpu.CompilerParams(
             collective_id=0, has_side_effects=True, vmem_limit_bytes=62 * 2**20

time: 76.7 us -> 74.8 us (0.975)
  Pallas kernels: 74 us -> 72.1 us
    pallas_call x1, Pallas kernels: 74 us -> 72.1 us  [march(): pl.pallas_call(functools.partial(march_kernel, n_dev, RUN), out_shape=jax...]
where the time goes in v5:
time: 74.8 us; the launch traced here: 74.6 us
  Pallas kernels  72.1 us (96%)
  local copies, waits for them, and re-layouts  1.87 us (2%)
    pallas_call x1, Pallas kernels, march(): pl.pallas_call(functools.partial(march_kernel, n_dev, RUN), out_shape=jax...  72.1 us
    unnamed x1, local copies, waits for them, and re-layouts  1.87 us

profile of v5, /device:TPU:25, one launch (start us, length us, event | category | flops | bytes accessed | tf_op | source)
XLA Modules:
  0.0 74.6 jit_solution(1950984348871445850)
XLA Ops:
  0.7 72.1 %march.1 = bf16[2,512,256]{2,1,0:T(8,128)(2,1)} custom-call(s32[1,6]{1,0:T(1,128)} %targets.1, s32[1,6]{1,0:T(1,128)} %delays.1, s32[1]{0:T(128)S(6)} %copy.9.counts, bf16[1,6,4,512,512]{4,3,2,1,0:T(8,128)(2,1)} %couplings.1, bf16[32,512,256]{2,1,0:T(8,128)(2,1)} %history.1, bf16[1,512,512]{2,1,0:T(8,128)(2,1)} %diag.1, bf16[2,512,256]{2,1,0:T(8,128)(2,1)} %incident.1), custom_call_target="tpu_custom_call" | custom-call | tf_op jit(solution)/shard_map/march/pallas_call | solution.py:354
  72.7 1.9 %copy.10 = bf16[2,512,256]{2,1,0:T(8,128)(2,1)} copy(bf16[2,512,256]{2,1,0:T(8,128)(2,1)} %march.1) | data formatting | bytes 1048576

commit v6 on v5

--- a/solution.py
+++ b/solution.py
@@ -21,9 +21,7 @@
 def march_kernel(
     n_dev,
     run,
-    targets,
-    delays,
-    counts,
+    table,
     couplings,
     history,
     diag,
@@ -50,6 +48,14 @@
     g = lax.axis_index("group")
     d = lax.axis_index("dev")
     slots = mats.shape[0]
+
+    def target(c):
+        return table[0, c]
+
+    def delay(c):
+        return table[0, slots + c]
+
+    count = table[0, 2 * slots]
     unk = mats.shape[2]
     halves = terms.shape[1]
     tiles = unk // TILE
@@ -166,10 +172,10 @@
         copy, _, hears = copy_of(t, h, r, kind, side)
         when(hears, copy.wait_recv)
 
-    live = [(jnp.int32(c) < counts[0]) for c in range(slots)]
+    live = [(jnp.int32(c) < count) for c in range(slots)]
 
     def weight(s, c):
-        return jnp.where(live[c] & (targets[0, c] == s), 1.0, 0.0).astype(jnp.float32)
+        return jnp.where(live[c] & (target(c) == s), 1.0, 0.0).astype(jnp.float32)
 
     weights = [[weight(s, c) for c in range(slots)] for s in range(11)]
 
@@ -198,7 +204,7 @@
         gather_terms(t, h, r, (3, 1, 2))
 
     def first_of(c):
-        return jnp.maximum(delays[0, c], 1) - 1
+        return jnp.maximum(delay(c), 1) - 1
 
     def products(shift, rows, over_halves):
         def taken(at):
@@ -265,7 +271,7 @@
     def out_copy(t, h):
         return pltpu.make_async_copy(result.at[t, h], out.at[t, :, pl.ds(h * LANES, LANES)], out_sem.at[t, h])
 
-    fresh = [jnp.where(delays[0, c] == 1, 1.0, 0.0).astype(jnp.float32) for c in range(slots)]
+    fresh = [jnp.where(delay(c) == 1, 1.0, 0.0).astype(jnp.float32) for c in range(slots)]
 
     def refresh(h, rows):
         lead = mats[:, 0, rows, :].reshape(slots * TILE, unk)
@@ -317,14 +323,12 @@
             refresh(h, tile_rows(r))
             launch(1, h, r)
 
-            @pl.when(r > 0)
-            def _():
-                join(1, h, r - 1)
-
+        @pl.loop(0, tiles)
+        def _(r):
+            join(1, h, r)
             if h:
                 pass_on(1, h - 1, r)
 
-        join(1, h, tiles - 1)
 
     @pl.loop(0, tiles)
     def _(r):
@@ -348,13 +352,14 @@
     _, slots, band, unk, _ = couplings.shape
     hist, _, exc = history.shape
     halves = exc // LANES
+    table = jnp.concatenate([targets, delays, counts[None]], axis=1)
     smem = pl.BlockSpec(memory_space=pltpu.SMEM)
     hbm = pl.BlockSpec(memory_space=pl.ANY)
     block = (unk, LANES)
     return pl.pallas_call(
         functools.partial(march_kernel, n_dev, RUN),
         out_shape=jax.ShapeDtypeStruct((STEPS, unk, exc), jnp.bfloat16),
-        in_specs=[smem, smem, smem, hbm, hbm, hbm, hbm],
+        in_specs=[smem, hbm, hbm, hbm, hbm],
         out_specs=hbm,
         scratch_shapes=[
             pltpu.VMEM((hist + 1,) + block, jnp.bfloat16),
@@ -376,10 +381,10 @@
             pltpu.SemaphoreType.DMA((STEPS, halves)),
         ],
         compiler_params=pltpu.CompilerParams(
-            collective_id=0, has_side_effects=True, vmem_limit_bytes=62 * 2**20
+            collective_id=0, has_side_effects=True, vmem_limit_bytes=53 * 2**20 + 2**17
         ),
         name="march",
-    )(targets, delays, counts, couplings, history, diag_inverse, incident)
+    )(table, couplings, history, diag_inverse, incident)
 
 
 def solution(mesh):

time: 74.8 us -> 72.4 us (0.968)
  Pallas kernels: 72.1 us -> 70.1 us
  local copies, waits for them, and re-layouts: 1.87 us -> 0.8 us
  other arithmetic: 0 us -> 0.75 us
    pallas_call x1, Pallas kernels: 72.1 us -> 70.1 us  [march(): pl.pallas_call(functools.partial(march_kernel, n_dev, RUN), out_shape=jax...]
    unnamed x1, local copies, waits for them, and re-layouts: 1.87 us -> 0.8 us
    concatenate x0 -> x1, other arithmetic: none -> 0.75 us  [march(): table = jnp.concatenate([targets, delays, counts[None]], axis=1)]
where the time goes in v6:
time: 72.4 us; the launch traced here: 72.3 us
  Pallas kernels  70.1 us (97%)
  local copies, waits for them, and re-layouts  0.8 us (1%)
  other arithmetic  0.75 us (1%)
    pallas_call x1, Pallas kernels, march(): pl.pallas_call(functools.partial(march_kernel, n_dev, RUN), out_shape=jax...  70.1 us

profile of v6, /device:TPU:25, one launch (start us, length us, event | category | flops | bytes accessed | tf_op | source)
XLA Modules:
  0.0 72.3 jit_solution(2486066084401470553)
XLA Ops:
  0.7 0.7 %pad_add_fusion.table = s32[1,13]{1,0:T(1,128)S(1)} fusion(s32[1,1]{1,0:T(1,128)} %bitcast.1, s32[1,6]{1,0:T(1,128)} %param.12, s32[1,6]{1,0:T(1,128)} %param.11), kind=kLoop, calls=%fused_computation | loop fusion | flops 26 | bytes 104 | tf_op jit(solution)/shard_map/concatenate | solution.py:355
  1.4 70.1 %march.1 = bf16[2,512,256]{2,1,0:T(8,128)(2,1)S(1)} custom-call(s32[1,13]{1,0:T(1,128)S(1)} %pad_add_fusion.table, bf16[1,6,4,512,512]{4,3,2,1,0:T(8,128)(2,1)} %couplings.1, bf16[32,512,256]{2,1,0:T(8,128)(2,1)} %history.1, bf16[1,512,512]{2,1,0:T(8,128)(2,1)} %diag.1, bf16[2,512,256]{2,1,0:T(8,128)(2,1)} %incident.1), custom_call_target="tpu_custom_call" | custom-call | tf_op jit(solution)/shard_map/march/pallas_call | solution.py:359
  71.5 0.8 %copy.10 = bf16[2,512,256]{2,1,0:T(8,128)(2,1)} copy(bf16[2,512,256]{2,1,0:T(8,128)(2,1)S(1)} %march.1) | data formatting | bytes 1048576

commit v7 on v6

--- a/solution.py
+++ b/solution.py
@@ -76,10 +76,9 @@
     skip_dev = d - jnp.where(at_start, 1, 0) + jnp.where(at_end, 1, 0)
     skips = crosses & (skip_dev >= 0) & (skip_dev < n_dev)
     gathers = crosses & jnp.logical_not(at_rim)
-    skip_into = jnp.where(at_rim, 2, jnp.where(even, 1, 3))
+    skip_into = jnp.where(even, 1, 3)
     side_into = jnp.where(even, 3, 1)
     near_side = jnp.where(at_start, 1, 0)
-    skip_into = jnp.where(at_rim, 2, jnp.where(even, 1, 3))
 
     def tile_rows(r):
         return pl.ds(pl.multiple_of(r * TILE, TILE), TILE)
@@ -237,10 +236,13 @@
     def pass_on(t, h, r):
         rows = tile_rows(r)
         arrive(t, h, r, CHIP)
-        arrive(t, h, r, SKIP)
-        add(t, h, r, skip_into, SKIP, skips)
-        arrive(t, h, r, SIDE)
-        add(t, h, r, side_into, SIDE, gathers)
+
+        @pl.when(gathers)
+        def _():
+            for kind, code in ((SKIP, skip_into), (SIDE, side_into)):
+                arrive(t, h, r, kind)
+                add(t, h, r, code, kind, None)
+
         for side in (near_side, 1 - near_side):
             code = 3 - 2 * side
             arrive(t, h, r, FAR, side)
@@ -256,9 +258,13 @@
         def _(r):
             rows = tile_rows(r)
             terms[t, h, 2, rows] = terms[t, h, 2, rows] + chip_box[t, h, 1, rows]
-            for kind, side, there in ((MIDDLE, 0, crosses), (SUM, 0, has_left), (SUM, 1, has_right)):
-                arrive(t, h, r, kind, side)
-                add(t, h, r, 2, kind + side, there)
+            for kind, side, there in ((SKIP, 0, skips & at_rim), (MIDDLE, 0, crosses), (SUM, 0, has_left), (SUM, 1, has_right)):
+
+                @pl.when(there)
+                def _():
+                    arrive(t, h, r, kind, side)
+                    add(t, h, r, 2, kind + side, None)
+
             right_side = (shine[t, rows, cols].astype(jnp.float32) - terms[t, h, 2, rows]).astype(jnp.bfloat16)
             solved[...] += jnp.dot(solve[:, rows], right_side, preferred_element_type=jnp.float32)
 
@@ -267,6 +273,13 @@
         out_copy(t, h).start()
         if t == 0:
             current_box[...] = current
+
+    def drain(t, h, kinds):
+        @pl.loop(0, tiles)
+        def _(r):
+            for kind, side in kinds:
+                copy, sends, _ = copy_of(t, h, r, kind, side, True)
+                when(sends, copy.wait_send)
 
     def out_copy(t, h):
         return pltpu.make_async_copy(result.at[t, h], out.at[t, :, pl.ds(h * LANES, LANES)], out_sem.at[t, h])
@@ -334,17 +347,18 @@
     def _(r):
         pass_on(1, halves - 1, r)
 
+    early = ((FAR, 0), (FAR, 1), (CHIP, 0), (JOIN, 0), (SKIP, 0))
+    late = ((SUM, 0), (SUM, 1), (MIDDLE, 0))
     for h in every:
+        drain(0, h, early + late)
+    for h in every[:-1]:
         solve_step(1, h)
+        drain(1, h, early + late)
+    drain(1, every[-1], early)
+    solve_step(1, every[-1])
+    drain(1, every[-1], late)
     for t in range(STEPS):
-        for h in range(halves):
-
-            @pl.loop(0, tiles)
-            def _(r):
-                for kind, side in ((FAR, 0), (FAR, 1), (SUM, 0), (SUM, 1), (CHIP, 0), (JOIN, 0), (SKIP, 0), (MIDDLE, 0)):
-                    copy, sends, _ = copy_of(t, h, r, kind, side, True)
-                    when(sends, copy.wait_send)
-
+        for h in every:
             out_copy(t, h).wait()
 
 

time: 72.4 us -> 72.1 us (level)
  no operation moved by 1% of the time
where the time goes in v7:
time: 72.1 us; the launch traced here: 72 us
  Pallas kernels  69.8 us (97%)
  local copies, waits for them, and re-layouts  0.8 us (1%)
  other arithmetic  0.75 us (1%)
    pallas_call x1, Pallas kernels, march(): pl.pallas_call(functools.partial(march_kernel, n_dev, RUN), out_shape=jax...  69.8 us

profile of v7, /device:TPU:25, one launch (start us, length us, event | category | flops | bytes accessed | tf_op | source)
XLA Modules:
  0.0 72.0 jit_solution(397742682131357588)
XLA Ops:
  0.7 0.7 %pad_add_fusion.table = s32[1,13]{1,0:T(1,128)S(1)} fusion(s32[1,1]{1,0:T(1,128)} %bitcast.1, s32[1,6]{1,0:T(1,128)} %param.12, s32[1,6]{1,0:T(1,128)} %param.11), kind=kLoop, calls=%fused_computation | loop fusion | flops 26 | bytes 104 | tf_op jit(solution)/shard_map/concatenate | solution.py:369
  1.4 69.8 %march.1 = bf16[2,512,256]{2,1,0:T(8,128)(2,1)S(1)} custom-call(s32[1,13]{1,0:T(1,128)S(1)} %pad_add_fusion.table, bf16[1,6,4,512,512]{4,3,2,1,0:T(8,128)(2,1)} %couplings.1, bf16[32,512,256]{2,1,0:T(8,128)(2,1)} %history.1, bf16[1,512,512]{2,1,0:T(8,128)(2,1)} %diag.1, bf16[2,512,256]{2,1,0:T(8,128)(2,1)} %incident.1), custom_call_target="tpu_custom_call" | custom-call | tf_op jit(solution)/shard_map/march/pallas_call | solution.py:373
  71.2 0.8 %copy.10 = bf16[2,512,256]{2,1,0:T(8,128)(2,1)} copy(bf16[2,512,256]{2,1,0:T(8,128)(2,1)S(1)} %march.1) | data formatting | bytes 1048576
